TPU v7x, 32 devices: a whole 2x2x4 slice. The times are simulated.
32 devices in a mesh: dp: 8 (over z, y), seq: 4 (over x, core).
Axes of the slice: x: 2, y: 2, z: 4, core: 2. Of those that a mesh axis runs over, the one named last changes fastest.
Arguments:
- patches: bfloat16 [24, 896, 768], P('dp', 'seq'), may hold values from -6 to 6
- cotangent: bfloat16 [24, 896, 768], P('dp', 'seq'), may hold values from -6 to 6
- time_ids: int32 [24, 896], P('dp', 'seq'), may hold values from 0 to 100
- freq_ids: int32 [24, 896], P('dp', 'seq'), may hold values from 0 to 11
- lengths: int32 [24], P('dp'), may hold values from 300 to 700, as said below
- qkv_weight: bfloat16 [768, 2304], replicated, may hold values from -0.21875 to 0.21875
- query_bias: float32 [768], replicated, may hold values from -3 to 3
- value_bias: float32 [768], replicated, may hold values from -3 to 3
- out_weight: bfloat16 [768, 768], replicated, may hold values from -0.875 to 0.875
- out_bias: float32 [768], replicated, may hold values from -3 to 3
- norm1_gain: float32 [768], replicated, may hold values from 0.25 to 1.75
- norm1_shift: float32 [768], replicated, may hold values from -3 to 3
- norm2_gain: float32 [768], replicated, may hold values from 0.25 to 1.75
- norm2_shift: float32 [768], replicated, may hold values from -3 to 3
- up_weight: bfloat16 [768, 3072], replicated, may hold values from -0.21875 to 0.21875
- up_bias: float32 [3072], replicated, may hold values from -3 to 3
- down_weight: bfloat16 [3072, 768], replicated, may hold values from -0.109375 to 0.109375
- down_bias: float32 [768], replicated, may hold values from -3 to 3
- time_table: float32 [101, 768], replicated, may hold values from -3 to 3
- freq_table: float32 [12, 768], replicated, may hold values from -3 to 3
Outputs:
- output: bfloat16 [24, 896, 768], P('dp', 'seq')
- d_patches: bfloat16 [24, 896, 768], P('dp', 'seq')
- grad_qkv_weight: float32 [768, 2304], P('dp')
- grad_query_bias: float32 [768], P('dp')
- grad_value_bias: float32 [768], P('dp')
- grad_out_weight: float32 [768, 768], P('dp')
- grad_out_bias: float32 [768], P('dp')
- grad_norm1_gain: float32 [768], P('dp')
- grad_norm1_shift: float32 [768], P('dp')
- grad_norm2_gain: float32 [768], P('dp')
- grad_norm2_shift: float32 [768], P('dp')
- grad_up_weight: float32 [768, 3072], P('dp')
- grad_up_bias: float32 [3072], P('dp')
- grad_down_weight: float32 [3072, 768], P('dp')
- grad_down_bias: float32 [768], P('dp')
- grad_time_table: float32 [101, 768], P(None, 'dp')
- grad_freq_table: float32 [12, 768], P(None, 'dp')
Inputs may be any that keep to these rules, and one draw needn't show every extreme that they name: `lengths`: at least one clip keeps exactly 700 patches.
All inputs are finite; a program needn't handle non-finite values.
Results may differ from a plain program's by a relative error of at most 0.015.
Values may be sent and summed in bfloat16 or wider, within the bound.
A program may use at most 192 MiB of HBM per device.

v0:
```python
import math

import jax
import jax.numpy as jnp
from jax import lax
from jax.sharding import PartitionSpec as P

HEADS = 12
MICRO = 3


EPS = 1e-06
NEGATIVE = -1000000000.0


def layer_norm(values, gain, shift):
    center = values - jnp.mean(values, -1, keepdims=True)
    spread = jnp.mean(center * center, -1, keepdims=True)
    return center * lax.rsqrt(spread + EPS) * gain + shift


def gelu_exact(values):
    return jax.nn.gelu(values, approximate=False)


def regroup(matrix, outer, inner):
    leading = matrix.shape[:-1]
    columns = matrix.shape[-1] // (outer * inner)
    moved = jnp.swapaxes(matrix.reshape(leading + (outer, inner, columns)), -3, -2)
    return moved.reshape(leading + (outer * inner * columns,))


def score_block(query, keys, key_valid):
    scale = 1.0 / math.sqrt(query.shape[-1])
    scores = jnp.einsum("qhd,khd->hqk", query, keys, preferred_element_type=jnp.float32) * scale
    return jnp.where(key_valid[None, None, :], scores, NEGATIVE)


def attend(item):
    query, keys, values, key_valid = item
    scores = score_block(query, keys, key_valid)
    highest = jnp.max(scores, -1, keepdims=True)
    powers = jnp.exp(scores - highest)
    total_mass = jnp.sum(powers, -1, keepdims=True)
    probs = powers / total_mass
    mixed = jnp.einsum(
        "hqk,khd->qhd", probs.astype(jnp.bfloat16), values, preferred_element_type=jnp.float32
    )
    return (mixed.astype(jnp.bfloat16), (highest + jnp.log(total_mass))[..., 0])


def attend_back(item):
    query, keys, values, key_valid, log_total, d_mixed = item
    scale = 1.0 / math.sqrt(query.shape[-1])
    scores = score_block(query, keys, key_valid)
    probs = jnp.exp(scores - log_total[..., None])
    d_probs = jnp.einsum("qhd,khd->hqk", d_mixed, values, preferred_element_type=jnp.float32)
    inner = jnp.sum(probs * d_probs, -1, keepdims=True)
    d_scores = (probs * (d_probs - inner)).astype(jnp.bfloat16)
    d_query = jnp.einsum("hqk,khd->qhd", d_scores, keys, preferred_element_type=jnp.float32) * scale
    d_keys = jnp.einsum("hqk,qhd->khd", d_scores, query, preferred_element_type=jnp.float32) * scale
    d_values = jnp.einsum(
        "hqk,qhd->khd", probs.astype(jnp.bfloat16), d_mixed, preferred_element_type=jnp.float32
    )
    return jnp.stack([d_query, d_keys, d_values], 1).astype(jnp.bfloat16)


def column_sums(values):
    return jnp.sum(values.astype(jnp.float32), (0, 1))


def micro_step(patch, cotan, time_part, freq_part, length_part, weights, start_row):
    (
        qkv_mat,
        qkv_shift,
        out_weight,
        out_bias,
        norm1_gain,
        norm1_shift,
        norm2_gain,
        norm2_shift,
        up_weight,
        up_bias,
        down_weight,
        down_bias,
        time_table,
        freq_table,
    ) = weights
    clip_count, row_count, features = patch.shape
    groups = lax.axis_size("seq")
    slot_count = row_count * groups
    group_cols = 3 * features // groups
    head_dim = features // HEADS
    heads_here = HEADS // groups
    highest = lax.Precision.HIGHEST
    positions = start_row + jnp.arange(row_count, dtype=jnp.int32)
    valid = (positions[None, :] < length_part[:, None]).astype(jnp.float32)
    key_valid = jnp.arange(slot_count, dtype=jnp.int32)[None, :] < length_part[:, None]
    time_hot = (time_part[..., None] == jnp.arange(time_table.shape[0], dtype=jnp.int32)).astype(
        jnp.float32
    )
    freq_hot = (freq_part[..., None] == jnp.arange(freq_table.shape[0], dtype=jnp.int32)).astype(
        jnp.float32
    )
    start = (
        patch.astype(jnp.float32)
        + jnp.einsum("crp,pd->crd", time_hot, time_table, precision=highest)
        + jnp.einsum("crp,pd->crd", freq_hot, freq_table, precision=highest)
    )
    normed = layer_norm(start, norm1_gain, norm1_shift).astype(jnp.bfloat16)
    joined = (
        jnp.einsum("crd,de->cre", normed, qkv_mat, preferred_element_type=jnp.float32) + qkv_shift
    ).astype(jnp.bfloat16)
    heads = lax.all_to_all(
        joined.reshape(clip_count, row_count, groups, group_cols),
        "seq",
        split_axis=2,
        concat_axis=1,
        tiled=True,
    )
    heads = heads.reshape(clip_count, slot_count, 3, heads_here, head_dim)
    query, keys, values = (heads[:, :, 0], heads[:, :, 1], heads[:, :, 2])
    mixed_heads, log_total = lax.map(attend, (query, keys, values, key_valid))
    mixed = lax.all_to_all(
        mixed_heads.reshape(clip_count, slot_count, heads_here * head_dim),
        "seq",
        split_axis=1,
        concat_axis=2,
        tiled=True,
    )
    after_attn = (
        start
        + jnp.einsum("crd,de->cre", mixed, out_weight, preferred_element_type=jnp.float32)
        + out_bias
    )
    normed_two = layer_norm(after_attn, norm2_gain, norm2_shift).astype(jnp.bfloat16)
    hidden = (
        jnp.einsum("crd,df->crf", normed_two, up_weight, preferred_element_type=jnp.float32)
        + up_bias
    )
    act = gelu_exact(hidden).astype(jnp.bfloat16)
    after_mlp = (
        after_attn
        + jnp.einsum("crf,fd->crd", act, down_weight, preferred_element_type=jnp.float32)
        + down_bias
    )
    output = (valid[..., None] * after_mlp).astype(jnp.bfloat16)
    d_after_mlp = valid[..., None] * cotan.astype(jnp.float32)
    d_branch = d_after_mlp.astype(jnp.bfloat16)
    grad_down = jnp.einsum("crf,crd->fd", act, d_branch, preferred_element_type=jnp.float32)
    grad_down_shift = column_sums(d_branch)
    d_act = jnp.einsum("crd,fd->crf", d_branch, down_weight, preferred_element_type=jnp.float32)
    d_hidden = jax.vjp(gelu_exact, hidden)[1](d_act)[0].astype(jnp.bfloat16)
    grad_up = jnp.einsum("crd,crf->df", normed_two, d_hidden, preferred_element_type=jnp.float32)
    grad_up_shift = column_sums(d_hidden)
    d_normed_two = jnp.einsum(
        "crf,df->crd", d_hidden, up_weight, preferred_element_type=jnp.float32
    )
    d_norm_in, grad_gain_two, grad_shift_two = jax.vjp(
        layer_norm, after_attn, norm2_gain, norm2_shift
    )[1](d_normed_two)
    d_after_attn = d_after_mlp + d_norm_in
    d_attn_out = d_after_attn.astype(jnp.bfloat16)
    grad_out = jnp.einsum("crd,cre->de", mixed, d_attn_out, preferred_element_type=jnp.float32)
    grad_out_shift = column_sums(d_attn_out)
    d_mixed = jnp.einsum(
        "cre,de->crd", d_attn_out, out_weight, preferred_element_type=jnp.float32
    ).astype(jnp.bfloat16)
    d_mixed_heads = lax.all_to_all(d_mixed, "seq", split_axis=2, concat_axis=1, tiled=True)
    d_mixed_heads = d_mixed_heads.reshape(clip_count, slot_count, heads_here, head_dim)
    d_heads = lax.map(attend_back, (query, keys, values, key_valid, log_total, d_mixed_heads))
    d_joined = lax.all_to_all(
        d_heads.reshape(clip_count, slot_count, 1, group_cols),
        "seq",
        split_axis=1,
        concat_axis=2,
        tiled=True,
    )
    d_joined = d_joined.reshape(clip_count, row_count, 3 * features)
    grad_joined = jnp.einsum("crd,cre->de", normed, d_joined, preferred_element_type=jnp.float32)
    grad_joined_shift = column_sums(d_joined)
    d_normed = jnp.einsum("cre,de->crd", d_joined, qkv_mat, preferred_element_type=jnp.float32)
    d_norm_first, grad_gain_one, grad_shift_one = jax.vjp(
        layer_norm, start, norm1_gain, norm1_shift
    )[1](d_normed)
    d_start = d_after_attn + d_norm_first
    grad_time = jnp.einsum("crp,crd->pd", time_hot, d_start, precision=highest)
    grad_freq = jnp.einsum("crp,crd->pd", freq_hot, d_start, precision=highest)
    grads = (
        grad_joined,
        grad_joined_shift,
        grad_out,
        grad_out_shift,
        grad_gain_one,
        grad_shift_one,
        grad_gain_two,
        grad_shift_two,
        grad_up,
        grad_up_shift,
        grad_down,
        grad_down_shift,
        grad_time,
        grad_freq,
    )
    return (output, d_start.astype(jnp.bfloat16), grads)


def finalize(grads, groups, features):
    (
        grad_joined,
        grad_joined_shift,
        grad_out,
        grad_out_shift,
        grad_gain_one,
        grad_shift_one,
        grad_gain_two,
        grad_shift_two,
        grad_up,
        grad_up_shift,
        grad_down,
        grad_down_shift,
        grad_time,
        grad_freq,
    ) = grads
    grad_qkv = regroup(grad_joined, groups, 3)
    bias_parts = regroup(grad_joined_shift, groups, 3).reshape(3, features)
    return (
        grad_qkv,
        bias_parts[0],
        bias_parts[2],
        grad_out,
        grad_out_shift,
        grad_gain_one,
        grad_shift_one,
        grad_gain_two,
        grad_shift_two,
        grad_up,
        grad_up_shift,
        grad_down,
        grad_down_shift,
        grad_time,
        grad_freq,
    )


def reduce_once(parts):
    return (
        lax.psum_scatter(parts[0], "dp", scatter_dimension=0, tiled=True),
        lax.psum_scatter(parts[1], "dp", scatter_dimension=0, tiled=True),
        lax.psum_scatter(parts[2], "dp", scatter_dimension=0, tiled=True),
        lax.psum_scatter(parts[3], "dp", scatter_dimension=0, tiled=True),
        lax.psum_scatter(parts[4], "dp", scatter_dimension=0, tiled=True),
        lax.psum_scatter(parts[5], "dp", scatter_dimension=0, tiled=True),
        lax.psum_scatter(parts[6], "dp", scatter_dimension=0, tiled=True),
        lax.psum_scatter(parts[7], "dp", scatter_dimension=0, tiled=True),
        lax.psum_scatter(parts[8], "dp", scatter_dimension=0, tiled=True),
        lax.psum_scatter(parts[9], "dp", scatter_dimension=0, tiled=True),
        lax.psum_scatter(parts[10], "dp", scatter_dimension=0, tiled=True),
        lax.psum_scatter(parts[11], "dp", scatter_dimension=0, tiled=True),
        lax.psum_scatter(parts[12], "dp", scatter_dimension=0, tiled=True),
        lax.psum_scatter(parts[13], "dp", scatter_dimension=1, tiled=True),
        lax.psum_scatter(parts[14], "dp", scatter_dimension=1, tiled=True),
    )


def sum_over_clip(parts):
    return (
        lax.psum(parts[0].astype(jnp.bfloat16), "seq").astype(jnp.float32),
        lax.psum(parts[1].astype(jnp.bfloat16), "seq").astype(jnp.float32),
        lax.psum(parts[2].astype(jnp.bfloat16), "seq").astype(jnp.float32),
        lax.psum(parts[3].astype(jnp.bfloat16), "seq").astype(jnp.float32),
        lax.psum(parts[4].astype(jnp.bfloat16), "seq").astype(jnp.float32),
        lax.psum(parts[5].astype(jnp.bfloat16), "seq").astype(jnp.float32),
        lax.psum(parts[6].astype(jnp.bfloat16), "seq").astype(jnp.float32),
        lax.psum(parts[7].astype(jnp.bfloat16), "seq").astype(jnp.float32),
        lax.psum(parts[8].astype(jnp.bfloat16), "seq").astype(jnp.float32),
        lax.psum(parts[9].astype(jnp.bfloat16), "seq").astype(jnp.float32),
        lax.psum(parts[10].astype(jnp.bfloat16), "seq").astype(jnp.float32),
        lax.psum(parts[11].astype(jnp.bfloat16), "seq").astype(jnp.float32),
        lax.psum(parts[12].astype(jnp.bfloat16), "seq").astype(jnp.float32),
        lax.psum(parts[13].astype(jnp.bfloat16), "seq").astype(jnp.float32),
        lax.psum(parts[14].astype(jnp.bfloat16), "seq").astype(jnp.float32),
    )


def shards(
    patches,
    cotangent,
    time_ids,
    freq_ids,
    lengths,
    qkv_weight,
    query_bias,
    value_bias,
    out_weight,
    out_bias,
    norm1_gain,
    norm1_shift,
    norm2_gain,
    norm2_shift,
    up_weight,
    up_bias,
    down_weight,
    down_bias,
    time_table,
    freq_table,
):
    groups = lax.axis_size("seq")
    features = patches.shape[2]
    start_row = lax.axis_index("seq") * patches.shape[1]
    qkv_mat = regroup(qkv_weight, 3, groups)
    full_shift = jnp.concatenate([query_bias, jnp.zeros_like(query_bias), value_bias])
    qkv_shift = regroup(full_shift, 3, groups)
    weights = (
        qkv_mat,
        qkv_shift,
        out_weight,
        out_bias,
        norm1_gain,
        norm1_shift,
        norm2_gain,
        norm2_shift,
        up_weight,
        up_bias,
        down_weight,
        down_bias,
        time_table,
        freq_table,
    )
    per_batch = patches.shape[0] // MICRO
    outputs = []
    d_pieces = []
    summed = None
    for index in range(MICRO):
        first = index * per_batch
        last = first + per_batch
        output, d_piece, grads = micro_step(
            patches[first:last],
            cotangent[first:last],
            time_ids[first:last],
            freq_ids[first:last],
            lengths[first:last],
            weights,
            start_row,
        )
        outputs.append(output)
        d_pieces.append(d_piece)
        summed = grads if summed is None else tuple((a + b for a, b in zip(summed, grads)))
    local_part = reduce_once(finalize(summed, groups, features))
    final = sum_over_clip(local_part)
    return (
        jnp.concatenate(outputs, 0),
        jnp.concatenate(d_pieces, 0),
        final[0],
        final[1],
        final[2],
        final[3],
        final[4],
        final[5],
        final[6],
        final[7],
        final[8],
        final[9],
        final[10],
        final[11],
        final[12],
        final[13],
        final[14],
    )


def solution(mesh):
    return jax.shard_map(
        shards,
        mesh=mesh,
        in_specs=(
            P("dp", "seq", None),
            P("dp", "seq", None),
            P("dp", "seq"),
            P("dp", "seq"),
            P("dp"),
            P(),
            P(),
            P(),
            P(),
            P(),
            P(),
            P(),
            P(),
            P(),
            P(),
            P(),
            P(),
            P(),
            P(),
            P(),
        ),
        out_specs=(
            P("dp", "seq", None),
            P("dp", "seq", None),
            P("dp", None),
            P("dp"),
            P("dp"),
            P("dp", None),
            P("dp"),
            P("dp"),
            P("dp"),
            P("dp"),
            P("dp"),
            P("dp", None),
            P("dp"),
            P("dp", None),
            P("dp"),
            P(None, "dp"),
            P(None, "dp"),
        ),
        check_vma=False,
    )
```

profile of v0, /device:TPU:0, one launch (start us, length us, event | category | flops | bytes accessed | tf_op | source)
XLA Modules:
  0.0 1185.3 jit_solution(14176737175925559739)
XLA Ops:
  12.1 5.8 copy.123
  36.8 4.4 fusion.18
  61.7 4.8 all-to-all-start
  83.2 4.4 all-to-all-start.4
  108.2 5.2 reduce.59
  115.7 4.4 all-to-all-start.3
  140.3 5.2 reduce.60
  151.2 5.2 reduce.58
  174.2 4.6 all-to-all-start.5
  190.2 10.9 multiply_convert_fusion.5
  201.1 8.4 multiply_convert_fusion.4
  226.5 9.6 multiply_convert_fusion.3
  236.1 5.3 convert_reduce_fusion
  241.4 5.1 fusion.240
  246.6 5.3 convert_reduce_fusion.2
  297.1 4.4 all-to-all-start.8
  304.6 9.7 multiply_reduce_fusion.2
  324.1 9.3 multiply_reduce_fusion.1
  333.4 6.2 fusion.84
  339.6 10.6 multiply_convert_fusion.2
  359.7 8.9 reduce.66
  371.1 4.5 all-to-all-start.7
  378.7 10.5 multiply_convert_fusion.1
  389.2 9.2 multiply_reduce_fusion
  398.4 10.4 multiply_convert_fusion
  418.6 8.9 reduce.64
  433.9 4.4 all-to-all-start.9
  442.3 5.4 fusion.81
  451.7 8.9 reduce.62
  467.3 4.7 reshape.1516
  476.2 4.5 reshape.1522
  484.9 4.5 reshape.1528
  504.0 8.0 copy.164
  512.0 6.4 copy.165
  518.4 8.0 copy.179
  532.2 5.3 add_add_fusion.1
  542.2 6.5 add_add_fusion
  552.7 5.1 fusion.62
  557.8 4.5 fusion.61
  562.2 4.7 fusion.60
  587.5 71.5 %reduce-scatter.19.cloned.1.call-done = f32[96,2304]{1,0:T(8,128)} async-done(((f32[768,2304]{1,0:T(8,128)}), f32[96,2304]{1,0:T(8,128)}) %reduce-scatter.19.cloned.1.call-update) | async-done | bytes 884752
  661.2 164.2 %reduce-scatter.13.cloned.1.call-done = f32[96,3072]{1,0:T(8,128)} async-done(((f32[768,3072]{1,0:T(8,128)}), f32[96,3072]{1,0:T(8,128)}) %reduce-scatter.13.cloned.1.call-update) | async-done | bytes 1179664 | tf_op jit(solution)/shard_map/reduce_scatter | solution.py:257
  827.6 164.2 %reduce-scatter.15.cloned.1.call-done = f32[384,768]{1,0:T(8,128)} async-done(((f32[3072,768]{1,0:T(8,128)}), f32[384,768]{1,0:T(8,128)}) %reduce-scatter.15.cloned.1.call-update) | async-done | bytes 1179664 | tf_op jit(solution)/shard_map/reduce_scatter | solution.py:259
  994.2 35.7 %all-reduce.9 = (bf16[768]{0:T(1024)(128)(2,1)S(1)}, bf16[768]{0:T(1024)(128)(2,1)S(1)}, bf16[768]{0:T(1024)(128)(2,1)S(1)}, bf16[768]{0:T(1024)(128)(2,1)S(1)},...) all-reduce(f32[768]{0:T(1024)S(1)} %squeeze.120, ...), channel_id=3, replica_groups=mesh['dp'=8,'seq'=4] {'dp'}, use_global_device_ids=true, to_apply=%region_38.39.clone | all-reduce | flops 9216 | bytes 55296
  1031.7 24.1 %reduce-scatter.21.cloned.1.call-done = f32[96,12]{1,0:T(8,128)} async-done(((f32[768,12]{1,0:T(8,128)}), f32[96,12]{1,0:T(8,128)}) %reduce-scatter.21.cloned.1.call-update) | async-done | bytes 4624
  1056.7 63.1 %reduce-scatter.17.cloned.1.call-done = f32[101,96]{0,1:T(8,128)} async-done(((f32[101,768]{0,1:T(8,128)}), f32[101,96]{0,1:T(8,128)}) %reduce-scatter.17.cloned.1.call-update) | async-done | bytes 38800 | tf_op jit(solution)/shard_map/reduce_scatter | solution.py:261
  1120.5 10.5 all-reduce.10
  1136.9 35.0 %all-reduce.14.cloned.1.call-done = (bf16[96,2304]{0,1:T(8,128)(2,1)}, bf16[96,768]{1,0:T(8,128)(2,1)}, bf16[96,3072]{1,0:T(8,128)(2,1)}, bf16[384,768]{1,0:T(8,128)(2,1)}) async-done(((bf16[96,2304]{0,1:T(8,128)(2,1)}, bf16[96,768]{1,0:T(8,128)(2,1)}, bf16[96,3072]{1,0:T(8,128)(2,1)}, bf16[384,768]{1,0:T(8,128)(2,1)}), (bf16[96,2304]{0,1:T(8,128)(2,1)}, bf16[96,768]{1,0:T(8,128)(2,1)}, ...) | async-done | bytes 1769488 | tf_op jit(solution)/shard_map/psum | solution.py:268
  (555 shorter events, 337.2 us)
Async XLA Ops:
  7.2 165.7 %copy-start = (bf16[768,768]{1,0:T(8,128)(2,1)S(1)}, bf16[768,768]{1,0:T(8,128)(2,1)}, u32[]{:S(2)}) copy-start(bf16[768,768]{1,0:T(8,128)(2,1)} %param.28) | copy-start | bytes 3538948
  8.0 9.8 copy-start.116
  8.0 26.4 %copy-start.118 = (s32[1,224]{1,0:T(1,128)}, s32[1,224]{1,0:T(1,128)S(1)}, u32[]{:S(2)}) copy-start(s32[1,224]{1,0:T(1,128)S(1)} %get-tuple-element.303) | copy-start | bytes 2692
  8.0 33.2 %copy-start.114 = (s32[1,224]{1,0:T(1,128)}, s32[1,224]{1,0:T(1,128)S(1)}, u32[]{:S(2)}) copy-start(s32[1,224]{1,0:T(1,128)S(1)} %get-tuple-element.304) | copy-start | bytes 2692
  8.8 26.1 %copy-start.112 = (s32[1,224]{1,0:T(1,128)}, s32[1,224]{1,0:T(1,128)S(1)}, u32[]{:S(2)}) copy-start(s32[1,224]{1,0:T(1,128)S(1)} %get-tuple-element.300) | copy-start | bytes 2692
  8.9 32.9 %copy-start.108 = (s32[1,224]{1,0:T(1,128)}, s32[1,224]{1,0:T(1,128)S(1)}, u32[]{:S(2)}) copy-start(s32[1,224]{1,0:T(1,128)S(1)} %get-tuple-element.301) | copy-start | bytes 2692
  11.8 161.0 %copy-start.7 = (f32[1,224,768]{2,1,0:T(8,128)}, f32[1,224,768]{2,1,0:T(8,128)S(1)}, u32[]{:S(2)}) copy-start(f32[1,224,768]{2,1,0:T(8,128)S(1)} %get-tuple-element.317) | copy-start | bytes 2064388
  11.9 10.5 copy-start.81
  12.1 10.2 copy-start.93
  30.2 31.5 %all-to-all-start.2 = ((bf16[1,224,4,576]{3,1,0,2:T(8,128)(2,1)}), bf16[1,224,4,576]{3,1,0,2:T(8,128)(2,1)}, u32[]{:S(2)}, u32[]{:S(2)}) async-start(bf16[1,224,4,576]{3,1,0,2:T(8,128)(2,1)} %copy.131), calls=%async_computation.2 | async-start | bytes 2293760 | tf_op jit(solution)/shard_map/all_to_all | solution.py:114
  36.5 152.4 %copy-start.9 = (f32[1,224,768]{2,1,0:T(8,128)}, f32[1,224,768]{2,1,0:T(8,128)S(1)}, u32[]{:S(2)}) copy-start(f32[1,224,768]{2,1,0:T(8,128)S(1)} %get-tuple-element.324) | copy-start | bytes 2064388
  61.7 21.5 %all-to-all-start = ((bf16[1,224,4,576]{3,1,0,2:T(8,128)(2,1)}), bf16[1,224,4,576]{3,1,0,2:T(8,128)(2,1)}, u32[]{:S(2)}, u32[]{:S(2)}) async-start(bf16[1,224,4,576]{3,1,0,2:T(8,128)(2,1)} %copy.125), calls=%async_computation | async-start | bytes 2293760 | tf_op jit(solution)/shard_map/all_to_all | solution.py:114
  83.2 32.6 %all-to-all-start.4 = ((bf16[1,224,4,576]{3,1,0,2:T(8,128)(2,1)}), bf16[1,224,4,576]{3,1,0,2:T(8,128)(2,1)}, u32[]{:S(2)}, u32[]{:S(2)}) async-start(bf16[1,224,4,576]{3,1,0,2:T(8,128)(2,1)} %copy.137), calls=%async_computation.4 | async-start | bytes 2293760 | tf_op jit(solution)/shard_map/all_to_all | solution.py:114
  115.7 43.0 %all-to-all-start.3 = ((bf16[4,2,21504]{2,1,0:T(2,128)(2,1)}), bf16[4,2,21504]{2,1,0:T(2,128)(2,1)}, u32[]{:S(2)}, u32[]{:S(2)}) async-start(bf16[4,2,21504]{2,1,0:T(2,128)(2,1)} %reshape.1517), calls=%async_computation.3 | async-start | bytes 688128 | tf_op jit(solution)/shard_map/all_to_all | solution.py:124
  156.4 16.4 %copy-start.80 = (f32[768]{0:T(1024)S(1)}, f32[768]{0:T(1024)}, u32[]{:S(2)}) copy-start(f32[768]{0:T(1024)} %param.29) | copy-start | bytes 9220
  158.7 15.5 %all-to-all-start.1 = ((bf16[4,2,21504]{2,1,0:T(2,128)(2,1)}), bf16[4,2,21504]{2,1,0:T(2,128)(2,1)}, u32[]{:S(2)}, u32[]{:S(2)}) async-start(bf16[4,2,21504]{2,1,0:T(2,128)(2,1)} %reshape.1511), calls=%async_computation.1 | async-start | bytes 688128 | tf_op jit(solution)/shard_map/all_to_all | solution.py:124
  174.2 43.2 %all-to-all-start.5 = ((bf16[4,2,21504]{2,1,0:T(2,128)(2,1)}), bf16[4,2,21504]{2,1,0:T(2,128)(2,1)}, u32[]{:S(2)}, u32[]{:S(2)}) async-start(bf16[4,2,21504]{2,1,0:T(2,128)(2,1)} %reshape.1523), calls=%async_computation.5 | async-start | bytes 688128 | tf_op jit(solution)/shard_map/all_to_all | solution.py:124
  188.9 12.1 %slice-start.3 = ((s8[4718592]{0:T(1024)(128)(4,1)}), s8[4194304]{0:T(1024)(128)(4,1)S(1)}, s32[]{:S(2)}) async-start(s8[4718592]{0:T(1024)(128)(4,1)} %bitcast.585), calls=%async_computation.28 | async-start | bytes 8388608
  189.7 11.4 copy-start.16
  190.2 10.9 slice-start.4
  190.2 19.3 %slice-start.7 = ((s8[4718592]{0:T(1024)(128)(4,1)}), s8[4194304]{0:T(1024)(128)(4,1)S(1)}, s32[]{:S(2)}) async-start(s8[4718592]{0:T(1024)(128)(4,1)} %bitcast.589), calls=%async_computation.32 | async-start | bytes 8388608
  225.6 10.5 copy-start.48
  226.2 28.3 %copy-start.11 = (f32[1,224,768]{2,1,0:T(8,128)}, f32[1,224,768]{2,1,0:T(8,128)S(1)}, u32[]{:S(2)}) copy-start(f32[1,224,768]{2,1,0:T(8,128)S(1)} %get-tuple-element.314) | copy-start | bytes 2064388
  236.1 10.4 copy-start.138
  241.4 10.4 slice-start.5
  256.6 28.0 %copy-start.50 = (bf16[1,224,768]{2,1,0:T(8,128)(2,1)}, bf16[1,224,768]{2,1,0:T(8,128)(2,1)S(1)}, u32[]{:S(2)}) copy-start(bf16[1,224,768]{2,1,0:T(8,128)(2,1)S(1)} %get-tuple-element.279) | copy-start | bytes 1032196
  272.0 25.1 %all-to-all-start.6 = ((bf16[4,2,21504]{2,1,0:T(2,128)(2,1)}), bf16[4,2,21504]{2,1,0:T(2,128)(2,1)}, u32[]{:S(2)}, u32[]{:S(2)}) async-start(bf16[4,2,21504]{2,1,0:T(2,128)(2,1)} %reshape.1513), calls=%async_computation.6 | async-start | bytes 688128 | tf_op jit(solution)/shard_map/all_to_all | solution.py:169
  276.1 309.8 %reduce-scatter.11.cloned.1.call-start = ((), (), s32[]{:S(2)}) async-start(), calls=%async_computation.18 | async-start | bytes 2654208 | tf_op jit(solution)/shard_map/reduce_scatter | solution.py:251
  282.2 10.5 copy-start.49
  297.1 17.3 %slice-start = ((s8[9633792]{0:T(1024)(128)(4,1)}), s8[1245184]{0:T(1024)(128)(4,1)S(1)}, s32[]{:S(2)}) async-start(s8[9633792]{0:T(1024)(128)(4,1)} %bitcast.517), calls=%async_computation.25 | async-start | bytes 2490368
  297.1 19.7 %all-to-all-start.8 = ((bf16[4,2,21504]{2,1,0:T(2,128)(2,1)}), bf16[4,2,21504]{2,1,0:T(2,128)(2,1)}, u32[]{:S(2)}, u32[]{:S(2)}) async-start(bf16[4,2,21504]{2,1,0:T(2,128)(2,1)} %reshape.1519), calls=%async_computation.8 | async-start | bytes 688128 | tf_op jit(solution)/shard_map/all_to_all | solution.py:169
  304.6 9.7 slice-start.1
  316.8 54.3 %all-to-all-start.10 = ((bf16[4,2,21504]{2,1,0:T(2,128)(2,1)}), bf16[4,2,21504]{2,1,0:T(2,128)(2,1)}, u32[]{:S(2)}, u32[]{:S(2)}) async-start(bf16[4,2,21504]{2,1,0:T(2,128)(2,1)} %reshape.1525), calls=%async_computation.10 | async-start | bytes 688128 | tf_op jit(solution)/shard_map/all_to_all | solution.py:169
  339.6 10.6 copy-start.27
  371.1 62.9 %all-to-all-start.7 = ((bf16[4,2,64512]{2,1,0:T(2,128)(2,1)}), bf16[4,2,64512]{2,1,0:T(2,128)(2,1)}, u32[]{:S(2)}, u32[]{:S(2)}) async-start(bf16[4,2,64512]{2,1,0:T(2,128)(2,1)} %reshape.1515), calls=%async_computation.7 | async-start | bytes 2064384 | tf_op jit(solution)/shard_map/all_to_all | solution.py:172
  378.7 10.5 copy-start.26
  433.9 29.1 %all-to-all-start.9 = ((bf16[4,2,64512]{2,1,0:T(2,128)(2,1)}), bf16[4,2,64512]{2,1,0:T(2,128)(2,1)}, u32[]{:S(2)}, u32[]{:S(2)}) async-start(bf16[4,2,64512]{2,1,0:T(2,128)(2,1)} %reshape.1521), calls=%async_computation.9 | async-start | bytes 2064384 | tf_op jit(solution)/shard_map/all_to_all | solution.py:172
  463.0 21.8 %all-to-all-start.11 = ((bf16[4,2,64512]{2,1,0:T(2,128)(2,1)}), bf16[4,2,64512]{2,1,0:T(2,128)(2,1)}, u32[]{:S(2)}, u32[]{:S(2)}) async-start(bf16[4,2,64512]{2,1,0:T(2,128)(2,1)} %reshape.1527), calls=%async_computation.11 | async-start | bytes 2064384 | tf_op jit(solution)/shard_map/all_to_all | solution.py:172
  467.3 191.7 %reduce-scatter.19.cloned.1.call-start = ((), (), s32[]{:S(2)}) async-start(), calls=%async_computation.22 | async-start | bytes 7962624
  526.4 299.0 %reduce-scatter.13.cloned.1.call-start = ((), (), s32[]{:S(2)}) async-start(), calls=%async_computation.19 | async-start | bytes 10616832 | tf_op jit(solution)/shard_map/reduce_scatter | solution.py:257
  537.5 454.2 %reduce-scatter.15.cloned.1.call-start = ((), (), s32[]{:S(2)}) async-start(), calls=%async_computation.20 | async-start | bytes 10616832 | tf_op jit(solution)/shard_map/reduce_scatter | solution.py:259
  548.9 506.9 %reduce-scatter.21.cloned.1.call-start = ((), (), s32[]{:S(2)}) async-start(), calls=%async_computation.23 | async-start | bytes 442368
  578.9 540.9 %reduce-scatter.17.cloned.1.call-start = ((), (), s32[]{:S(2)}) async-start(), calls=%async_computation.21 | async-start | bytes 442368 | tf_op jit(solution)/shard_map/reduce_scatter | solution.py:261
  581.6 590.3 %all-reduce.14.cloned.1.call-start = ((), (), s32[]{:S(2)}) async-start(), calls=%async_computation.24 | async-start | bytes 3833856 | tf_op jit(solution)/shard_map/psum | solution.py:268
  661.2 369.4 %copy-start.61 = (bf16[1,224,768]{2,1,0:T(8,128)(2,1)S(1)}, bf16[1,224,768]{2,1,0:T(8,128)(2,1)}, u32[]{:S(2)}) copy-start(bf16[1,224,768]{2,1,0:T(8,128)(2,1)} %get-tuple-element.250) | copy-start | bytes 1032196
  661.2 369.4 %copy-start.62 = (bf16[1,224,768]{2,1,0:T(8,128)(2,1)S(1)}, bf16[1,224,768]{2,1,0:T(8,128)(2,1)}, u32[]{:S(2)}) copy-start(bf16[1,224,768]{2,1,0:T(8,128)(2,1)} %get-tuple-element.280) | copy-start | bytes 1032196
  661.2 369.4 %copy-start.63 = (bf16[1,224,768]{2,1,0:T(8,128)(2,1)S(1)}, bf16[1,224,768]{2,1,0:T(8,128)(2,1)}, u32[]{:S(2)}) copy-start(bf16[1,224,768]{2,1,0:T(8,128)(2,1)} %get-tuple-element.282) | copy-start | bytes 1032196
  1131.7 46.6 %copy-start.1 = (bf16[768,768]{1,0:T(8,128)(2,1)S(1)}, bf16[768,768]{1,0:T(8,128)(2,1)}, u32[]{:S(2)}) copy-start(bf16[768,768]{1,0:T(8,128)(2,1)} %param.28) | copy-start | bytes 3538948
  (119 other events, 431.1 us)
Sparse Core Ops, SparseCore 0:
  297.2 72.2 reduce-scatter.10
  526.6 132.4 reduce-scatter.18
  663.0 162.3 reduce-scatter.12
  829.3 162.4 reduce-scatter.14
  995.2 60.5 reduce-scatter.20
  1059.3 60.4 reduce-scatter.16
  1123.7 48.1 all-reduce.13
where the time goes:
time: 1200 us; the launch traced here: 1190 us
  waiting for transfers between devices  522 us (44%)
  matrix products  218 us (18%)
  local copies, waits for them, and re-layouts  204 us (17%)
  other arithmetic  123 us (10%)
  starting transfers between devices  53.4 us (4%)
  blocking collectives  46.2 us (4%)
  between operations  17.8 us (1%)
    reduce_scatter x1, waiting for transfers between devices, reduce_once(): lax.psum_scatter(parts[9], 'dp', scatter_dimension=0, tiled=True)  164 us
    reduce_scatter x1, waiting for transfers between devices, reduce_once(): lax.psum_scatter(parts[11], 'dp', scatter_dimension=0, tiled=True)  164 us
    unnamed x9, waiting for transfers between devices  95.7 us
    unnamed x337, local copies, waits for them, and re-layouts  90.6 us
    reduce_scatter x1, waiting for transfers between devices, reduce_once(): lax.psum_scatter(parts[13], 'dp', scatter_dimension=1, tiled=True)  63.1 us
    unnamed x13, other arithmetic  53.4 us
    unnamed x1, blocking collectives  35.7 us
    psum x1, waiting for transfers between devices, sum_over_clip(): lax.psum(parts[0].astype(jnp.bfloat16), 'seq').astype(jnp.float32)  35 us
  transfers between devices with their start and end apart: 19, of which 6 were waited for; matrix products, arithmetic and copies ran while one was open for 38% of the time, Pallas kernels for 0%

commit v1 on v0

v1 whole, which is shorter than its diff:
```python
import functools
import math

import jax
import jax.numpy as jnp
from jax import lax
from jax.experimental import pallas as pl
from jax.experimental.pallas import tpu as pltpu
from jax.sharding import PartitionSpec as P

HEADS = 12
KEEP_MAX = 700
EPS = 1e-06
NEGATIVE = -1000000000.0
FREQ_ROW = 104
TABLE_ROWS = 128
SMALL_ROWS = 16 + TABLE_ROWS
F32 = jnp.float32
BF16 = jnp.bfloat16
NN = (((1,), (0,)), ((), ()))
NT = (((1,), (1,)), ((), ()))
TN = (((0,), (0,)), ((), ()))
MIB = 1 << 20


def mm(left, right, dims=NN):
    return lax.dot_general(left, right, dims, preferred_element_type=F32)


def params(limit=60):
    return pltpu.CompilerParams(vmem_limit_bytes=limit * MIB)


def row_sum(values):
    return jnp.sum(values, 0, keepdims=True)


def normalize(values):
    center = values - jnp.mean(values, -1, keepdims=True)
    rstd = lax.rsqrt(jnp.mean(center * center, -1, keepdims=True) + EPS)
    return center * rstd, rstd


def norm_back(d_out, gain, xhat, rstd):
    u = d_out * gain
    inner = jnp.mean(u * xhat, -1, keepdims=True)
    return rstd * (u - jnp.mean(u, -1, keepdims=True) - xhat * inner)


def split_high_low(values):
    high = values.astype(BF16)
    return high, (values - high.astype(F32)).astype(BF16)


def one_hot(time_row, freq_row):
    spot = lax.broadcasted_iota(jnp.int32, (TABLE_ROWS, time_row.shape[1]), 0)
    hit = (spot == time_row) | (spot == freq_row + FREQ_ROW)
    return jnp.where(hit, 1.0, 0.0).astype(BF16)


def project_body(groups, patch, time_ids, freq_ids, time_table, freq_table, gain, shift, weight, bias, x_out, n_out, heads_out, table):
    features = patch.shape[2]
    width = features // groups

    @pl.when(pl.program_id(0) == 0)
    def _():
        full = jnp.zeros((TABLE_ROWS, features), F32)
        table_f32 = x_out.at[0, 0:TABLE_ROWS]
        table_f32[...] = full
        x_out[0, 0:time_table.shape[0], :] = time_table[...]
        x_out[0, FREQ_ROW:FREQ_ROW + freq_table.shape[0], :] = freq_table[...]
        high, low = split_high_low(x_out[0, 0:TABLE_ROWS, :])
        table[0:TABLE_ROWS, :] = high
        table[TABLE_ROWS:, :] = low

    hot = one_hot(time_ids[0], freq_ids[0])
    x = patch[0].astype(F32) + mm(jnp.concatenate([hot, hot], 0), table[...], TN)
    x_out[0] = x
    xhat, _ = normalize(x)
    normed = (xhat * gain[...] + shift[...]).astype(BF16)
    n_out[0] = normed
    for part in range(3):
        cols = slice(part * features, (part + 1) * features)
        out = (mm(normed, weight[:, cols]) + bias[:, cols]).astype(BF16)
        for g in range(groups):
            heads_out[g, 0, :, part * width:(part + 1) * width] = out[:, g * width:(g + 1) * width]


def project(patch, time_ids, freq_ids, time_table, freq_table, gain, shift, weight, bias, groups):
    clips, rows, features = patch.shape
    width = features // groups
    whole = lambda a: pl.BlockSpec(a.shape, lambda c: (0,) * a.ndim)
    per_clip = lambda *tail: pl.BlockSpec((1,) + tail, lambda c: (c,) + (0,) * len(tail))
    return pl.pallas_call(
        functools.partial(project_body, groups),
        grid=(clips,),
        in_specs=[per_clip(rows, features), per_clip(1, rows), per_clip(1, rows)]
        + [whole(a) for a in (time_table, freq_table, gain, shift, weight, bias)],
        out_specs=[per_clip(rows, features), per_clip(rows, features), pl.BlockSpec((groups, 1, rows, 3 * width), lambda c: (0, c, 0, 0))],
        out_shape=[
            jax.ShapeDtypeStruct((clips, rows, features), F32),
            jax.ShapeDtypeStruct((clips, rows, features), BF16),
            jax.ShapeDtypeStruct((groups, clips, rows, 3 * width), BF16),
        ],
        scratch_shapes=[pltpu.VMEM((2 * TABLE_ROWS, features), BF16)],
        compiler_params=params(),
    )(patch, time_ids, freq_ids, time_table, freq_table, gain, shift, weight, bias)


def attend_body(used, head_dim, block, lengths, heads, mixed_out, log_out):
    groups, _, rows, width3 = heads.shape
    width = width3 // 3
    here = width // head_dim
    length = lengths[pl.program_id(0)]
    joined = heads[...].reshape(groups * rows, width3)[0:used]
    query = joined[:, 0:width] * BF16(1.0 / math.sqrt(head_dim))
    keys = joined[:, width:2 * width]
    values = joined[:, 2 * width:]
    lane = lax.broadcasted_iota(jnp.int32, (1, width), 1) // head_dim
    wide_lane = lax.broadcasted_iota(jnp.int32, (block, 128), 1)
    key_ok = lax.broadcasted_iota(jnp.int32, (1, used), 1) < length
    pieces = []
    logs = []
    for first in range(0, used, block):
        q_block = query[first:first + block]
        mixed = jnp.zeros((block, width), F32)
        log_wide = jnp.zeros((block, 128), F32)
        for h in range(here):
            q_head = jnp.where(lane == h, q_block, BF16(0))
            scores = jnp.where(key_ok, mm(q_head, keys, NT), NEGATIVE)
            highest = jnp.max(scores, -1, keepdims=True)
            powers = jnp.exp(scores - highest)
            total = jnp.sum(powers, -1, keepdims=True)
            out = mm(powers.astype(BF16), values) * (1.0 / total)
            mixed = mixed + jnp.where(lane == h, out, 0.0)
            log_wide = jnp.where(wide_lane == h, highest + jnp.log(total), log_wide)
        pieces.append(mixed.astype(BF16))
        logs.append(log_wide)
    tail = groups * rows - used
    pieces.append(jnp.zeros((tail, width), BF16))
    mixed_out[...] = jnp.concatenate(pieces, 0).reshape(mixed_out.shape)
    log_out[0] = jnp.concatenate(logs, 0).T[0:8]


def attend(heads, lengths, head_dim, used, block):
    groups, clips, rows, width3 = heads.shape
    width = width3 // 3
    return pl.pallas_call(
        functools.partial(attend_body, used, head_dim, block),
        grid_spec=pltpu.PrefetchScalarGridSpec(
            num_scalar_prefetch=1,
            grid=(clips,),
            in_specs=[pl.BlockSpec((groups, 1, rows, width3), lambda c, s: (0, c, 0, 0))],
            out_specs=[
                pl.BlockSpec((groups, 1, rows, width), lambda c, s: (0, c, 0, 0)),
                pl.BlockSpec((1, 8, used), lambda c, s: (c, 0, 0)),
            ],
        ),
        out_shape=[
            jax.ShapeDtypeStruct((groups, clips, rows, width), BF16),
            jax.ShapeDtypeStruct((clips, 8, used), F32),
        ],
        compiler_params=params(),
    )(lengths, heads)


def middle_body(clips, limits, x_in, mixed_in, cot, out_weight, out_bias, gain, shift, up, up_bias, down, down_bias,
                out_ref, d_mixed_ref, d_x1_ref, g_down_t, g_up, g_out, small, up_bias_grad,
                mixed, x1, n2, n2_t, dm, dm_t, acc, d_n2, act_all, d_hidden_all):
    step = pl.program_id(0)
    groups, total, width = mixed_in.shape
    rows = total // clips
    features = x_in.shape[1]

    def valid_rows(c):
        return lax.broadcasted_iota(jnp.int32, (rows, 1), 0) < limits[c]

    @pl.when(step == 0)
    def _():
        small[...] = jnp.zeros_like(small)
        for c in range(clips):
            span = slice(c * rows, (c + 1) * rows)
            for g in range(groups):
                mixed[span, g * width:(g + 1) * width] = mixed_in[g, span, :]
            after = x_in[span] + (mm(mixed[span], out_weight[...]) + out_bias[...])
            x1[span] = after
            xhat, _ = normalize(after)
            n2[span] = (xhat * gain[...] + shift[...]).astype(BF16)
            dm[span] = jnp.where(valid_rows(c), cot[span], BF16(0))
        n2_t[...] = n2[...].T
        dm_t[...] = dm[...].T
        acc[...] = jnp.zeros_like(acc)
        d_n2[...] = jnp.zeros_like(d_n2)
        small[7:8, :] = row_sum(dm[...].astype(F32))

    bias_sum = None
    for c in range(clips):
        span = slice(c * rows, (c + 1) * rows)
        hidden = mm(n2[span], up[...]) + up_bias[...]
        half = 0.5 * (1.0 + lax.erf(hidden * (1.0 / math.sqrt(2.0))))
        act = (hidden * half).astype(BF16)
        slope = half + hidden * jnp.exp(hidden * hidden * -0.5) * (1.0 / math.sqrt(2.0 * math.pi))
        d_hidden = (slope * mm(dm[span], down[...], NT)).astype(BF16)
        act_all[span] = act
        d_hidden_all[span] = d_hidden
        acc[span] += mm(act, down[...])
        d_n2[span] += mm(d_hidden, up[...], NT)
        part = row_sum(d_hidden.astype(F32))
        bias_sum = part if bias_sum is None else bias_sum + part
    up_bias_grad[...] = bias_sum
    g_down_t[...] = mm(dm_t[...], act_all[...]).astype(BF16)
    g_up[...] = mm(n2_t[...], d_hidden_all[...]).astype(BF16)

    @pl.when(step == pl.num_programs(0) - 1)
    def _():
        gain_sum = jnp.zeros((1, features), F32)
        shift_sum = jnp.zeros((1, features), F32)
        bias_out = jnp.zeros((1, features), F32)
        for c in range(clips):
            span = slice(c * rows, (c + 1) * rows)
            ok = valid_rows(c)
            after = x1[span]
            out_ref[span] = jnp.where(ok, after + (acc[span] + down_bias[...]), 0.0).astype(BF16)
            xhat, rstd = normalize(after)
            d_norm = d_n2[span]
            gain_sum += row_sum(d_norm * xhat)
            shift_sum += row_sum(d_norm)
            d_x1 = dm[span].astype(F32) + norm_back(d_norm, gain[...], xhat, rstd)
            d_x1_ref[span] = d_x1
            d_a = d_x1.astype(BF16)
            n2[span] = d_a
            bias_out += row_sum(d_a.astype(F32))
            d_mixed = mm(d_a, out_weight[...], NT).astype(BF16)
            for g in range(groups):
                d_mixed_ref[g, span, :] = d_mixed[:, g * width:(g + 1) * width]
        g_out[...] = mm(mixed[...].T, n2[...]).astype(BF16)
        small[2:3, :] = bias_out
        small[5:6, :] = gain_sum
        small[6:7, :] = shift_sum


def middle(limits, x, mixed, cot, out_weight, out_bias, gain, shift, up, up_bias, down, down_bias, clips, tile):
    total, features = x.shape
    groups, _, width = mixed.shape
    hidden = up.shape[1]
    whole = lambda a: pl.BlockSpec(a.shape, lambda j, s: (0,) * len(a.shape))
    outs = [
        jax.ShapeDtypeStruct((total, features), BF16),
        jax.ShapeDtypeStruct((groups, total, width), BF16),
        jax.ShapeDtypeStruct((total, features), F32),
        jax.ShapeDtypeStruct((features, hidden), BF16),
        jax.ShapeDtypeStruct((features, hidden), BF16),
        jax.ShapeDtypeStruct((features, features), BF16),
        jax.ShapeDtypeStruct((8, features), F32),
        jax.ShapeDtypeStruct((1, hidden), F32),
    ]
    cols = lambda height: pl.BlockSpec((height, tile), lambda j, s: (0, j))
    return pl.pallas_call(
        functools.partial(middle_body, clips),
        grid_spec=pltpu.PrefetchScalarGridSpec(
            num_scalar_prefetch=1,
            grid=(hidden // tile,),
            in_specs=[whole(x), whole(mixed), whole(cot), whole(out_weight), whole(out_bias), whole(gain), whole(shift),
                      cols(features), cols(1), pl.BlockSpec((tile, features), lambda j, s: (j, 0)), whole(down_bias)],
            out_specs=[whole(outs[0]), whole(outs[1]), whole(outs[2]), cols(features), cols(features), whole(outs[5]), whole(outs[6]), cols(1)],
            scratch_shapes=[
                pltpu.VMEM((total, features), BF16),
                pltpu.VMEM((total, features), F32),
                pltpu.VMEM((total, features), BF16),
                pltpu.VMEM((features, total), BF16),
                pltpu.VMEM((total, features), BF16),
                pltpu.VMEM((features, total), BF16),
                pltpu.VMEM((total, features), F32),
                pltpu.VMEM((total, features), F32),
                pltpu.VMEM((total, tile), BF16),
                pltpu.VMEM((total, tile), BF16),
            ],
        ),
        out_shape=outs,
        compiler_params=params(),
    )(limits, x, mixed, cot, out_weight, out_bias, gain, shift, up, up_bias, down, down_bias)


def attend_back_body(used, head_dim, block, lengths, heads, d_mixed_in, logs, d_heads):
    groups, _, rows, width3 = heads.shape
    width = width3 // 3
    here = width // head_dim
    length = lengths[pl.program_id(0)]
    scale = BF16(1.0 / math.sqrt(head_dim))
    joined = heads[...].reshape(groups * rows, width3)[0:used]
    d_mixed = d_mixed_in[...].reshape(groups * rows, width)[0:used]
    query = joined[:, 0:width] * scale
    keys = joined[:, width:2 * width]
    values = joined[:, 2 * width:]
    keys_t = (keys * scale).T
    lane = lax.broadcasted_iota(jnp.int32, (1, width), 1) // head_dim
    key_ok = lax.broadcasted_iota(jnp.int32, (used, 1), 0) < length
    d_keys = jnp.zeros((used, width), F32)
    d_values = jnp.zeros((used, width), F32)
    d_query_t = []
    for first in range(0, used, block):
        last = min(first + block, used)
        q_block = query[first:last]
        m_block = d_mixed[first:last]
        d_q_parts = []
        for h in range(here):
            q_head = jnp.where(lane == h, q_block, BF16(0))
            m_head = jnp.where(lane == h, m_block, BF16(0))
            scores = jnp.where(key_ok, mm(keys, q_head, NT), NEGATIVE)
            probs = jnp.exp(scores - logs[0, h:h + 1, first:last])
            d_values = d_values + mm(probs.astype(BF16), m_head)
            weighted = probs * mm(values, m_head, NT)
            d_scores = (weighted - probs * row_sum(weighted)).astype(BF16)
            d_keys = d_keys + mm(d_scores, q_head)
            d_q_parts.append(mm(keys_t[h * head_dim:(h + 1) * head_dim], d_scores))
        d_query_t.append(jnp.concatenate(d_q_parts, 0))
    d_query = jnp.concatenate(d_query_t, 1).T
    tail = jnp.zeros((groups * rows - used, width), BF16)
    for part, value in enumerate((d_query, d_keys, d_values)):
        full = jnp.concatenate([value.astype(BF16), tail], 0)
        d_heads[:, 0, :, part * width:(part + 1) * width] = full.reshape(groups, rows, width)


def attend_back(heads, d_mixed, logs, lengths, head_dim, used, block):
    groups, clips, rows, width3 = heads.shape
    width = width3 // 3
    spec = lambda cols: pl.BlockSpec((groups, 1, rows, cols), lambda c, s: (0, c, 0, 0))
    return pl.pallas_call(
        functools.partial(attend_back_body, used, head_dim, block),
        grid_spec=pltpu.PrefetchScalarGridSpec(
            num_scalar_prefetch=1,
            grid=(clips,),
            in_specs=[spec(width3), spec(width), pl.BlockSpec((1, 8, used), lambda c, s: (c, 0, 0))],
            out_specs=spec(width3),
        ),
        out_shape=jax.ShapeDtypeStruct((groups, clips, rows, width3), BF16),
        compiler_params=params(),
    )(lengths, heads, d_mixed, logs)


def finish_body(clips, d_heads, weight, normed, x_in, d_x1, time_ids, freq_ids, gain, small_in, d_patch, g_qkv, small, joined, high_low, hot):
    groups, total, width3 = d_heads.shape
    width = width3 // 3
    rows = total // clips
    features = x_in.shape[1]
    for part in range(3):
        for g in range(groups):
            first = part * features + g * width
            joined[:, first:first + width] = d_heads[g, :, part * width:(part + 1) * width]
    small[0:8, :] = small_in[...]
    small[8:16, :] = jnp.zeros((8, features), F32)
    gain_sum = jnp.zeros((1, features), F32)
    shift_sum = jnp.zeros((1, features), F32)
    query_sum = jnp.zeros((1, features), F32)
    value_sum = jnp.zeros((1, features), F32)
    for c in range(clips):
        span = slice(c * rows, (c + 1) * rows)
        d_norm = mm(joined[span], weight[...], NT)
        query_sum += row_sum(joined[span, 0:features].astype(F32))
        value_sum += row_sum(joined[span, 2 * features:].astype(F32))
        xhat, rstd = normalize(x_in[span])
        gain_sum += row_sum(d_norm * xhat)
        shift_sum += row_sum(d_norm)
        d_x = d_x1[span] + norm_back(d_norm, gain[...], xhat, rstd)
        high, low = split_high_low(d_x)
        d_patch[span] = high
        high_low[span, 0:features] = high
        high_low[span, features:] = low
    normed_t = normed[...].T
    for part in range(3):
        cols = slice(part * features, (part + 1) * features)
        g_qkv[:, cols] = mm(normed_t, joined[:, cols]).astype(BF16)
    tables = jnp.zeros((TABLE_ROWS, 2 * features), F32)
    for c in range(clips):
        tables = tables + mm(one_hot(time_ids[c], freq_ids[c]), high_low[c * rows:(c + 1) * rows])
    small[16:, :] = tables[:, 0:features] + tables[:, features:]
    small[0:1, :] = query_sum
    small[1:2, :] = value_sum
    small[3:4, :] = gain_sum
    small[4:5, :] = shift_sum


def finish(d_heads, weight, normed, x, d_x1, time_ids, freq_ids, gain, small, clips):
    total, features = x.shape
    return pl.pallas_call(
        functools.partial(finish_body, clips),
        out_shape=[
            jax.ShapeDtypeStruct((total, features), BF16),
            jax.ShapeDtypeStruct((features, 3 * features), BF16),
            jax.ShapeDtypeStruct((SMALL_ROWS, features), F32),
        ],
        scratch_shapes=[
            pltpu.VMEM((total, 3 * features), BF16),
            pltpu.VMEM((total, 2 * features), BF16),
            pltpu.VMEM((8, 128), F32),
        ],
        compiler_params=params(),
    )(d_heads, weight, normed, x, d_x1, time_ids, freq_ids, gain, small)


def exchange(array):
    return lax.all_to_all(array, "seq", split_axis=0, concat_axis=0, tiled=True)


def reduce_all(g_qkv, g_out, g_up, g_down_t, small, up_bias_grad):
    shares = lax.axis_size("dp")
    features = small.shape[1]
    hidden = up_bias_grad.shape[1]
    repeat = hidden // features
    chunks = up_bias_grad.reshape(shares, repeat, features // shares)
    small = small.at[8:8 + repeat].set(jnp.swapaxes(chunks, 0, 1).reshape(repeat, features))

    def total(part, axis):
        return lax.psum(lax.psum_scatter(part, "dp", scatter_dimension=axis, tiled=True), "seq").astype(F32)

    small = total(small, 1)
    up_bias = small[8:8 + repeat].reshape(hidden // shares)
    return (
        total(g_qkv, 0), small[0], small[1], total(g_out, 0), small[2], small[3], small[4], small[5], small[6],
        total(g_up, 0), up_bias, total(g_down_t, 1).T, small[7],
        small[16:16 + 101], small[16 + FREQ_ROW:16 + FREQ_ROW + 12],
    )


def shards(
    patches,
    cotangent,
    time_ids,
    freq_ids,
    lengths,
    qkv_weight,
    query_bias,
    value_bias,
    out_weight,
    out_bias,
    norm1_gain,
    norm1_shift,
    norm2_gain,
    norm2_shift,
    up_weight,
    up_bias,
    down_weight,
    down_bias,
    time_table,
    freq_table,
):
    groups = lax.axis_size("seq")
    clips, rows, features = patches.shape
    head_dim = features // HEADS
    width = features // groups
    total = clips * rows
    used = min(-(-KEEP_MAX // 16) * 16, rows * groups)
    limits = lengths - lax.axis_index("seq") * rows
    line = lambda v: v.reshape(1, -1)
    bias = line(jnp.concatenate([query_bias, jnp.zeros_like(query_bias), value_bias]))
    time_rows = time_ids.reshape(clips, 1, rows)
    freq_rows = freq_ids.reshape(clips, 1, rows)
    x, normed, heads = project(
        patches, time_rows, freq_rows, time_table, freq_table, line(norm1_gain), line(norm1_shift), qkv_weight, bias, groups
    )
    heads = exchange(heads)
    mixed, logs = attend(heads, lengths, head_dim, used, used // 4)
    mixed = exchange(mixed)
    x = x.reshape(total, features)
    output, d_mixed, d_x1, g_down_t, g_up, g_out, small, up_bias_grad = middle(
        limits, x, mixed.reshape(groups, total, width), cotangent.reshape(total, features), out_weight, line(out_bias),
        line(norm2_gain), line(norm2_shift), up_weight, line(up_bias), down_weight, line(down_bias), clips, 512
    )
    d_mixed = exchange(d_mixed.reshape(groups, clips, rows, width))
    d_heads = attend_back(heads, d_mixed, logs, lengths, head_dim, used, 256)
    d_heads = exchange(d_heads)
    d_patch, g_qkv, small = finish(
        d_heads.reshape(groups, total, 3 * width), qkv_weight, normed.reshape(total, features), x, d_x1, time_rows, freq_rows,
        line(norm1_gain), small, clips
    )
    shape = patches.shape
    return (output.reshape(shape), d_patch.reshape(shape)) + reduce_all(g_qkv, g_out, g_up, g_down_t, small, up_bias_grad)


def solution(mesh):
    clip_spec, row_spec, one = P("dp", "seq", None), P("dp", "seq"), P("dp")
    matrix = P("dp", None)
    return jax.shard_map(
        shards,
        mesh=mesh,
        in_specs=(clip_spec, clip_spec, row_spec, row_spec, one) + (P(),) * 15,
        out_specs=(clip_spec, clip_spec, matrix, one, one, matrix, one, one, one, one, one, matrix, one, matrix, one, P(None, "dp"), P(None, "dp")),
        check_vma=False,
    )
```

time: 1200 us -> 626 us (0.52); the launches traced: 1190 us -> 625 us
  matrix products: 218 us -> 0 us
  local copies, waits for them, and re-layouts: 204 us -> 31.5 us
  waiting for transfers between devices: 522 us -> 352 us
  other arithmetic: 123 us -> 5.71 us
  Pallas kernels: 0 us -> 95.9 us
  blocking collectives: 46.2 us -> 122 us
  starting transfers between devices: 53.4 us -> 3.95 us
    dot_general x66 -> x0, matrix products: 218 us -> none  [the longest x3 28.9 us: micro_step(): jnp.einsum('crd,df->crf', normed_two, up_weight, preferred_element_type=j...]
    reduce_scatter x4 -> x3, waiting for transfers between devices: 391 us -> 238 us  [total(): lax.psum_scatter(part, 'dp', scatter_dimension=axis, tiled=True)]
    all_to_all x0 -> x3, blocking collectives: none -> 110 us  [exchange(): return lax.all_to_all(array, 'seq', split_axis=0, concat_axis=0, tiled=True)]
    pallas_call x0 -> x5, Pallas kernels: none -> 95.9 us  [the longest x1 36.3 us: middle(): pl.pallas_call(functools.partial(middle_body, clips), grid_spec=pltpu.Pre...]
    unnamed x337 -> x26, local copies, waits for them, and re-layouts: 90.6 us -> 14.8 us
    unnamed x13 -> x0, other arithmetic: 53.4 us -> none
    all_to_all x12 -> x1, starting transfers between devices: 52.5 us -> 3.53 us  [exchange(): return lax.all_to_all(array, 'seq', split_axis=0, concat_axis=0, tiled=True)]
    convert_element_type x24 -> x3, other arithmetic: 52.7 us -> 3.81 us  [total(): lax.psum(lax.psum_scatter(part, 'dp', scatter_dimension=axis, tiled=True)...]
  transfers between devices with their start and end apart: 19 -> 7, of which waited for: 6 -> 6; matrix products, arithmetic and copies ran while one was open for 38% -> 2% of each run, Pallas kernels for 0% -> 5%
where the time goes in v1:
time: 626 us; the launch traced here: 625 us
  waiting for transfers between devices  352 us (56%)
  blocking collectives  122 us (19%)
  Pallas kernels  95.9 us (15%)
  local copies, waits for them, and re-layouts  31.5 us (5%)
  between operations  14.3 us (2%)
    reduce_scatter x3, waiting for transfers between devices, total(): lax.psum_scatter(part, 'dp', scatter_dimension=axis, tiled=True)  238 us
    all_to_all x3, blocking collectives, exchange(): return lax.all_to_all(array, 'seq', split_axis=0, concat_axis=0, tiled=True)  110 us
    unnamed x8, waiting for transfers between devices  67.2 us
    pallas_call x1, Pallas kernels, middle(): pl.pallas_call(functools.partial(middle_body, clips), grid_spec=pltpu.Pre...  36.3 us
    psum x1, waiting for transfers between devices, total(): lax.psum(lax.psum_scatter(part, 'dp', scatter_dimension=axis, tiled=True)...  33.8 us
    pallas_call x1, Pallas kernels, attend_back(): pl.pallas_call(functools.partial(attend_back_body, used, head_dim, block)...  20.5 us
    pallas_call x1, Pallas kernels, attend(): pl.pallas_call(functools.partial(attend_body, used, head_dim, block), gri...  17.5 us
    unnamed x26, local copies, waits for them, and re-layouts  14.8 us
  transfers between devices with their start and end apart: 7, of which 6 were waited for; matrix products, arithmetic and copies ran while one was open for 2% of the time, Pallas kernels for 5%

profile of v1, /device:TPU:0, one launch (start us, length us, event | category | flops | bytes accessed | tf_op | source)
XLA Modules:
  0.0 625.0 jit_solution(4621295719664642952)
XLA Ops:
  7.2 1.3 reshape.124.time_ids
  8.5 1.3 reshape.125.freq_ids
  9.7 1.3 reshape.126.gain
  11.0 1.3 reshape.127.shift
  12.3 0.7 pad_maximum_fusion
  13.0 0.6 reshape.128.bias
  13.6 8.4 %shard_map.323 = (f32[3,224,768]{2,1,0:T(8,128)}, bf16[3,224,768]{2,1,0:T(8,128)(2,1)}, bf16[4,3,224,576]{3,2,1,0:T(8,128)(2,1)}) custom-call(bf16[3,224,768]{2,1,0:T(8,128)(2,1)} %patch.1, s32[3,1,224]{2,1,0:T(1,128)} %reshape.124.time_ids, s32[3,1,224]{2,1,0:T(1,128)} %reshape.125.freq_ids, f32[101,768]{1,0:T(8,128)} %time_table.1, f32[12,768]{1,0:T(8,128)} %freq_table.1, ...), custom_call_target="tpu_custom_call" | custom-call | tf_op jit(solution)/shard_map/pallas_call | solution.py:94
  22.0 46.2 %all_to_all.20.heads = bf16[4,3,224,576]{3,2,1,0:T(8,128)(2,1)} all-to-all(bf16[4,3,224,576]{3,2,1,0:T(8,128)(2,1)} %get-tuple-element.46), channel_id=1, replica_groups=mesh['dp'=8,'seq'=4] {'seq'}, dimensions={0} | all-to-all | bytes 6193152 | tf_op jit(solution)/shard_map/all_to_all | solution.py:402
  68.2 17.5 %shard_map.324 = (bf16[4,3,224,192]{3,2,1,0:T(8,128)(2,1)}, f32[3,8,704]{2,1,0:T(8,128)}) custom-call(s32[3]{0:T(128)} %lengths.3, bf16[4,3,224,576]{3,2,1,0:T(8,128)(2,1)} %all_to_all.20.heads), custom_call_target="tpu_custom_call" | custom-call | tf_op jit(solution)/shard_map/pallas_call | solution.py:148
  85.8 2.5 copy.40
  88.3 3.5 all-to-all-start.1
  92.1 0.6 reshape.132.out_bias
  92.7 0.6 reshape.133.gain
  93.2 0.6 reshape.134.shift
  93.8 0.6 reshape.136.down_bias
  94.4 0.5 broadcast_subtract_fusion.limits
  94.9 12.7 %all-to-all-done.1 = bf16[4,3,224,192]{2,3,1,0:T(8,128)(2,1)S(1)} async-done(((bf16[4,3,224,192]{2,3,1,0:T(8,128)(2,1)}), bf16[4,3,224,192]{2,3,1,0:T(8,128)(2,1)S(1)}, u32[]{:S(2)}, u32[]{:S(2)}) %all-to-all-start.1) | async-done | bytes 1032224 | tf_op jit(solution)/shard_map/all_to_all | solution.py:402
  107.7 1.5 copy.41
  109.2 36.3 %shard_map.325 = (bf16[672,768]{1,0:T(8,128)(2,1)}, bf16[4,672,192]{2,1,0:T(8,128)(2,1)}, f32[672,768]{1,0:T(8,128)}, bf16[768,3072]{1,0:T(8,128)(2,1)}, bf16[76...) custom-call(s32[3]{0:T(128)} %broadcast_subtract_fusion.limits, ...), custom_call_target="tpu_custom_call" | custom-call | tf_op jit(solution)/shard_map/pallas_call | solution.py:258
  145.4 6.7 %copy.49 = bf16[768,3072]{0,1:T(8,128)(2,1)} copy(bf16[768,3072]{1,0:T(8,128)(2,1)} %get-tuple-element.60) | data formatting | bytes 9437184
  152.2 0.7 reduce-scatter.12.cloned.1.call-update
  153.0 0.7 reduce-scatter.14.cloned.1.call-update
  153.7 0.6 copy-done
  154.3 0.7 copy.42
  155.0 18.3 %all_to_all.21 = bf16[4,3,224,192]{2,3,1,0:T(8,128)(2,1)S(1)} all-to-all(bf16[4,3,224,192]{2,3,1,0:T(8,128)(2,1)S(1)} %copy.42), channel_id=1, replica_groups=mesh['dp'=8,'seq'=4] {'seq'}, dimensions={0} | all-to-all | bytes 2064384 | tf_op jit(solution)/shard_map/all_to_all | solution.py:402
  173.3 1.5 copy.43.d_mixed_in
  174.8 20.5 %shard_map.326 = bf16[4,3,224,576]{3,2,1,0:T(8,128)(2,1)} custom-call(s32[3]{0:T(128)} %lengths.3, bf16[4,3,224,576]{3,2,1,0:T(8,128)(2,1)} %all_to_all.20.heads, bf16[4,3,224,192]{3,2,1,0:T(8,128)(2,1)} %copy.43.d_mixed_in, f32[3,8,704]{2,1,0:T(8,128)} %get-tuple-element.50.logs), custom_call_target="tpu_custom_call" | custom-call | tf_op jit(solution)/shard_map/pallas_call | solution.py:328
  195.3 45.6 %all_to_all.22 = bf16[4,3,224,576]{3,2,1,0:T(8,128)(2,1)} all-to-all(bf16[4,3,224,576]{3,2,1,0:T(8,128)(2,1)} %shard_map.326), channel_id=1, replica_groups=mesh['dp'=8,'seq'=4] {'seq'}, dimensions={0} | all-to-all | bytes 6193152 | tf_op jit(solution)/shard_map/all_to_all | solution.py:402
  240.9 13.1 %shard_map.327 = (bf16[672,768]{1,0:T(8,128)(2,1)}, bf16[768,2304]{1,0:T(8,128)(2,1)}, f32[144,768]{1,0:T(8,128)}) custom-call(bf16[4,672,576]{2,1,0:T(8,128)(2,1)} %bitcast.34, bf16[768,2304]{1,0:T(8,128)(2,1)} %weight.3, bf16[672,768]{1,0:T(8,128)(2,1)} %bitcast.42, f32[672,768]{1,0:T(8,128)} %bitcast.36, f32[672,768]{1,0:T(8,128)} %get-tuple-element.52.d_x1, ...), custom_call_target="tpu_custom_call" | custom-call | tf_op jit(solution)/shard_map/pallas_call | solution.py:385
  254.1 0.5 broadcast.18
  254.7 0.7 reduce.5
  255.6 1.2 copy.47
  256.9 2.1 copy.50
  259.0 57.7 %reduce-scatter.12.cloned.1.call-done = bf16[96,768]{1,0:T(8,128)(2,1)} async-done(((bf16[768,768]{1,0:T(8,128)(2,1)}), bf16[96,768]{1,0:T(8,128)(2,1)}) %reduce-scatter.12.cloned.1.call-update) | async-done | bytes 147472 | tf_op jit(solution)/shard_map/reduce_scatter | solution.py:414
  316.7 98.1 %reduce-scatter.14.cloned.1.call-done = bf16[96,3072]{1,0:T(8,128)(2,1)} async-done(((bf16[768,3072]{1,0:T(8,128)(2,1)}), bf16[96,3072]{1,0:T(8,128)(2,1)}) %reduce-scatter.14.cloned.1.call-update) | async-done | bytes 589840 | tf_op jit(solution)/shard_map/reduce_scatter | solution.py:414
  414.8 82.5 %reduce-scatter.10.cloned.1.call-done = bf16[96,2304]{1,0:T(8,128)(2,1)} async-done(((bf16[768,2304]{1,0:T(8,128)(2,1)}), bf16[96,2304]{1,0:T(8,128)(2,1)}) %reduce-scatter.10.cloned.1.call-update) | async-done | bytes 442384 | tf_op jit(solution)/shard_map/reduce_scatter | solution.py:414
  497.2 65.7 %reduce-scatter.16.cloned.1.call-done = f32[96,144]{1,0:T(8,128)} async-done(((f32[768,144]{1,0:T(8,128)}), f32[96,144]{1,0:T(8,128)}) %reduce-scatter.16.cloned.1.call-update) | async-done | bytes 55312
  563.0 1.0 copy.48
  563.9 11.7 %psum.36 = f32[144,96]{1,0:T(8,128)S(1)} all-reduce(f32[144,96]{1,0:T(8,128)S(1)} %copy.48), channel_id=1, replica_groups=mesh['dp'=8,'seq'=4] {'seq'}, use_global_device_ids=true, to_apply=%region_3.0 | all-reduce | flops 13824 | bytes 110592 | tf_op jit(solution)/shard_map/psum | solution.py:414
  575.7 0.6 slice.71
  576.3 0.7 reshape.144
  577.0 0.7 copy.46
  577.7 0.5 slice_bitcast_fusion
  578.2 33.8 %all-reduce.3.cloned.1.call-done = (bf16[384,768]{0,1:T(8,128)(2,1)}, bf16[96,2304]{1,0:T(8,128)(2,1)}, bf16[96,768]{1,0:T(8,128)(2,1)}, bf16[96,3072]{1,0:T(8,128)(2,1)}) async-done(((bf16[384,768]{0,1:T(8,128)(2,1)}, bf16[96,2304]{1,0:T(8,128)(2,1)}, bf16[96,768]{1,0:T(8,128)(2,1)}, bf16[96,3072]{1,0:T(8,128)(2,1)}), (bf16[384,768]{0,1:T(8,128)(2,1)}, bf16[96,2304]{1,0:T(8,128)(2,1)}, ...) | async-done | bytes 1769488 | tf_op jit(solution)/shard_map/psum | solution.py:414
  612.1 1.7 convert_element_type.11
  613.8 2.3 copy.45
  616.1 1.0 convert_element_type.10
  617.1 1.1 convert_element_type.12
  (37 shorter events, 0.8 us)
Async XLA Ops:
  85.7 6.3 %copy-start.5 = (f32[768]{0:T(1024)S(1)}, f32[768]{0:T(1024)}, u32[]{:S(2)}) copy-start(f32[768]{0:T(1024)} %param.31) | copy-start | bytes 9220
  85.7 6.9 %copy-start.6 = (f32[768]{0:T(1024)S(1)}, f32[768]{0:T(1024)}, u32[]{:S(2)}) copy-start(f32[768]{0:T(1024)} %param.34) | copy-start | bytes 9220
  85.8 7.5 %copy-start.7 = (f32[768]{0:T(1024)S(1)}, f32[768]{0:T(1024)}, u32[]{:S(2)}) copy-start(f32[768]{0:T(1024)} %param.35) | copy-start | bytes 9220
  85.8 8.1 %copy-start.8 = (f32[768]{0:T(1024)S(1)}, f32[768]{0:T(1024)}, u32[]{:S(2)}) copy-start(f32[768]{0:T(1024)} %param.39) | copy-start | bytes 9220
  85.8 8.7 %copy-start.9 = (s32[3]{0:T(128)S(1)}, s32[3]{0:T(128)}, u32[]{:S(2)}) copy-start(s32[3]{0:T(128)} %lengths.3) | copy-start | bytes 40
  88.3 19.4 %all-to-all-start.1 = ((bf16[4,3,224,192]{2,3,1,0:T(8,128)(2,1)}), bf16[4,3,224,192]{2,3,1,0:T(8,128)(2,1)S(1)}, u32[]{:S(2)}, u32[]{:S(2)}) async-start(bf16[4,3,224,192]{2,3,1,0:T(8,128)(2,1)} %copy.40), calls=%async_computation.1 | async-start | bytes 2359296 | tf_op jit(solution)/shard_map/all_to_all | solution.py:402
  91.8 165.0 %reduce-scatter.18.cloned.1.call-start = ((), (), s32[]{:S(2)}) async-start(), calls=%async_computation.13 | async-start | bytes 5308416
  152.2 164.5 %reduce-scatter.12.cloned.1.call-start = ((), (), s32[]{:S(2)}) async-start(), calls=%async_computation.10 | async-start | bytes 1327104 | tf_op jit(solution)/shard_map/reduce_scatter | solution.py:414
  153.0 261.8 %reduce-scatter.14.cloned.1.call-start = ((), (), s32[]{:S(2)}) async-start(), calls=%async_computation.11 | async-start | bytes 5308416 | tf_op jit(solution)/shard_map/reduce_scatter | solution.py:414
  153.0 1.3 copy-start
  153.7 343.5 %reduce-scatter.10.cloned.1.call-start = ((), (), s32[]{:S(2)}) async-start(), calls=%async_computation.9 | async-start | bytes 3981312 | tf_op jit(solution)/shard_map/reduce_scatter | solution.py:414
  254.0 0.7 copy-start.4
  254.0 1.6 copy-start.2
  254.1 308.9 %reduce-scatter.16.cloned.1.call-start = ((), (), s32[]{:S(2)}) async-start(), calls=%async_computation.12 | async-start | bytes 884736
  256.8 355.3 %all-reduce.3.cloned.1.call-start = ((), (), s32[]{:S(2)}) async-start(), calls=%async_computation.14 | async-start | bytes 3538944 | tf_op jit(solution)/shard_map/psum | solution.py:414
  612.1 4.1 copy-start.3
  612.1 5.0 copy-start.1
Sparse Core Ops, SparseCore 0:
  152.3 96.3 reduce-scatter.17
  252.7 63.9 reduce-scatter.11
  320.3 94.3 reduce-scatter.13
  418.2 78.9 reduce-scatter.9
  500.9 61.9 reduce-scatter.15
  566.2 45.8 all-reduce.2

commit v2 on v1

--- a/solution.py
+++ b/solution.py
@@ -14,7 +14,7 @@
 NEGATIVE = -1000000000.0
 FREQ_ROW = 104
 TABLE_ROWS = 128
-SMALL_ROWS = 16 + TABLE_ROWS
+SMALL_ROWS = 32 + TABLE_ROWS
 F32 = jnp.float32
 BF16 = jnp.bfloat16
 NN = (((1,), (0,)), ((), ()))
@@ -164,13 +164,14 @@
     )(lengths, heads)
 
 
-def middle_body(clips, limits, x_in, mixed_in, cot, out_weight, out_bias, gain, shift, up, up_bias, down, down_bias,
-                out_ref, d_mixed_ref, d_x1_ref, g_down_t, g_up, g_out, small, up_bias_grad,
+def middle_body(clips, shares, limits, x_in, mixed_in, cot, out_weight, out_bias, gain, shift, up, up_bias, down, down_bias,
+                out_ref, d_mixed_ref, d_x1_ref, g_down_a, g_down_b, g_up_a, g_up_b, g_out, small, up_bias_grad,
                 mixed, x1, n2, n2_t, dm, dm_t, acc, d_n2, act_all, d_hidden_all):
     step = pl.program_id(0)
     groups, total, width = mixed_in.shape
     rows = total // clips
     features = x_in.shape[1]
+    share = features // shares
 
     def valid_rows(c):
         return lax.broadcasted_iota(jnp.int32, (rows, 1), 0) < limits[c]
@@ -208,8 +209,30 @@
         part = row_sum(d_hidden.astype(F32))
         bias_sum = part if bias_sum is None else bias_sum + part
     up_bias_grad[...] = bias_sum
-    g_down_t[...] = mm(dm_t[...], act_all[...]).astype(BF16)
-    g_up[...] = mm(n2_t[...], d_hidden_all[...]).astype(BF16)
+    tile = up.shape[1]
+    heights = g_down_a.shape[3], g_down_b.shape[2]
+    reach = g_down_a.shape[4]
+    for core in range(2):
+        first = core * (features // 2)
+        out = mm(dm_t[first:first + features // 2], act_all[...]).astype(BF16)
+        for d in range(tile // reach):
+            cols = slice(d * reach, (d + 1) * reach)
+            for half_x in range(2):
+                g_down_a[d, core, half_x] = out[half_x * heights[0]:(half_x + 1) * heights[0], cols]
+            g_down_b[d, core] = out[2 * heights[0]:, cols]
+    g_up_tile = mm(n2_t[...], d_hidden_all[...]).astype(BF16)
+
+    @pl.when(step % 2 == 0)
+    def _():
+        wide = tile // 2
+        for d in range(shares):
+            for half_x in range(2):
+                g_up_a[d, 0, half_x] = g_up_tile[d * share:(d + 1) * share, half_x * wide:(half_x + 1) * wide]
+
+    @pl.when(step % 2 == 1)
+    def _():
+        for d in range(shares):
+            g_up_b[d, 0] = g_up_tile[d * share:(d + 1) * share]
 
     @pl.when(step == pl.num_programs(0) - 1)
     def _():
@@ -233,36 +256,50 @@
             d_mixed = mm(d_a, out_weight[...], NT).astype(BF16)
             for g in range(groups):
                 d_mixed_ref[g, span, :] = d_mixed[:, g * width:(g + 1) * width]
-        g_out[...] = mm(mixed[...].T, n2[...]).astype(BF16)
+        out = mm(mixed[...].T, n2[...]).astype(BF16)
+        for d in range(shares):
+            for core in range(2):
+                g_out[d, core] = out[d * share:(d + 1) * share, core * (features // 2):(core + 1) * (features // 2)]
         small[2:3, :] = bias_out
         small[5:6, :] = gain_sum
         small[6:7, :] = shift_sum
 
 
-def middle(limits, x, mixed, cot, out_weight, out_bias, gain, shift, up, up_bias, down, down_bias, clips, tile):
+def middle(limits, x, mixed, cot, out_weight, out_bias, gain, shift, up, up_bias, down, down_bias, clips, tile, shares):
     total, features = x.shape
     groups, _, width = mixed.shape
     hidden = up.shape[1]
+    share, reach, half = features // shares, hidden // shares, features // 2
+    spread = max(tile // reach, 1)
     whole = lambda a: pl.BlockSpec(a.shape, lambda j, s: (0,) * len(a.shape))
     outs = [
         jax.ShapeDtypeStruct((total, features), BF16),
         jax.ShapeDtypeStruct((groups, total, width), BF16),
         jax.ShapeDtypeStruct((total, features), F32),
-        jax.ShapeDtypeStruct((features, hidden), BF16),
-        jax.ShapeDtypeStruct((features, hidden), BF16),
-        jax.ShapeDtypeStruct((features, features), BF16),
+        jax.ShapeDtypeStruct((shares, 2, 2, half // 4, reach), BF16),
+        jax.ShapeDtypeStruct((shares, 2, half // 2, reach), BF16),
+        jax.ShapeDtypeStruct((shares, 2, 2, share, hidden // 8), BF16),
+        jax.ShapeDtypeStruct((shares, 2, share, hidden // 4), BF16),
+        jax.ShapeDtypeStruct((shares, 2, share, half), BF16),
         jax.ShapeDtypeStruct((8, features), F32),
         jax.ShapeDtypeStruct((1, hidden), F32),
     ]
     cols = lambda height: pl.BlockSpec((height, tile), lambda j, s: (0, j))
+    if tile >= reach:
+        down_spec = lambda *mid: pl.BlockSpec((spread,) + mid + (reach,), lambda j, s: (j,) + (0,) * (len(mid) + 1))
+    else:
+        down_spec = lambda *mid: pl.BlockSpec((1,) + mid + (tile,), lambda j, s: (0,) * (len(mid) + 1) + (j,))
     return pl.pallas_call(
-        functools.partial(middle_body, clips),
+        functools.partial(middle_body, clips, shares),
         grid_spec=pltpu.PrefetchScalarGridSpec(
             num_scalar_prefetch=1,
             grid=(hidden // tile,),
             in_specs=[whole(x), whole(mixed), whole(cot), whole(out_weight), whole(out_bias), whole(gain), whole(shift),
                       cols(features), cols(1), pl.BlockSpec((tile, features), lambda j, s: (j, 0)), whole(down_bias)],
-            out_specs=[whole(outs[0]), whole(outs[1]), whole(outs[2]), cols(features), cols(features), whole(outs[5]), whole(outs[6]), cols(1)],
+            out_specs=[whole(outs[0]), whole(outs[1]), whole(outs[2]), down_spec(2, 2, half // 4), down_spec(2, half // 2),
+                       pl.BlockSpec((shares, 1, 2, share, tile // 2), lambda j, s: (0, j // 2, 0, 0, 0)),
+                       pl.BlockSpec((shares, 1, share, tile), lambda j, s: (0, j // 2, 0, 0)),
+                       whole(outs[7]), whole(outs[8]), cols(1)],
             scratch_shapes=[
                 pltpu.VMEM((total, features), BF16),
                 pltpu.VMEM((total, features), F32),
@@ -338,17 +375,19 @@
     )(lengths, heads, d_mixed, logs)
 
 
-def finish_body(clips, d_heads, weight, normed, x_in, d_x1, time_ids, freq_ids, gain, small_in, d_patch, g_qkv, small, joined, high_low, hot):
+def finish_body(clips, shares, d_heads, weight, normed, x_in, d_x1, time_ids, freq_ids, gain, small_in, up_bias_grad,
+                d_patch, g_qkv_a, g_qkv_b, packed, joined, high_low, small):
     groups, total, width3 = d_heads.shape
     width = width3 // 3
     rows = total // clips
     features = x_in.shape[1]
+    share = features // shares
     for part in range(3):
         for g in range(groups):
             first = part * features + g * width
             joined[:, first:first + width] = d_heads[g, :, part * width:(part + 1) * width]
     small[0:8, :] = small_in[...]
-    small[8:16, :] = jnp.zeros((8, features), F32)
+    small[8:, :] = jnp.zeros((small.shape[0] - 8, features), F32)
     gain_sum = jnp.zeros((1, features), F32)
     shift_sum = jnp.zeros((1, features), F32)
     query_sum = jnp.zeros((1, features), F32)
@@ -367,58 +406,264 @@
         high_low[span, 0:features] = high
         high_low[span, features:] = low
     normed_t = normed[...].T
-    for part in range(3):
-        cols = slice(part * features, (part + 1) * features)
-        g_qkv[:, cols] = mm(normed_t, joined[:, cols]).astype(BF16)
+    half = 3 * features // 2
+    wide = g_qkv_a.shape[4]
+    for core in range(2):
+        out = mm(normed_t, joined[:, core * half:(core + 1) * half]).astype(BF16)
+        for d in range(shares):
+            span = slice(d * share, (d + 1) * share)
+            for half_x in range(2):
+                g_qkv_a[d, core, half_x] = out[span, half_x * wide:(half_x + 1) * wide]
+            g_qkv_b[d, core] = out[span, 2 * wide:]
     tables = jnp.zeros((TABLE_ROWS, 2 * features), F32)
     for c in range(clips):
         tables = tables + mm(one_hot(time_ids[c], freq_ids[c]), high_low[c * rows:(c + 1) * rows])
-    small[16:, :] = tables[:, 0:features] + tables[:, features:]
+    small[16:16 + TABLE_ROWS, :] = tables[:, 0:features] + tables[:, features:]
     small[0:1, :] = query_sum
     small[1:2, :] = value_sum
     small[3:4, :] = gain_sum
     small[4:5, :] = shift_sum
-
-
-def finish(d_heads, weight, normed, x, d_x1, time_ids, freq_ids, gain, small, clips):
+    repeat = up_bias_grad.shape[1] // features
+    height = packed.shape[2]
+    if share != packed.shape[3]:
+        packed[...] = jnp.zeros_like(packed)
+    for d in range(shares):
+        for r in range(repeat):
+            first = (d * repeat + r) * share
+            small[8 + r:9 + r, d * share:(d + 1) * share] = up_bias_grad[:, first:first + share]
+        for core in range(2):
+            packed[d, core, :, 0:share] = small[core * height:(core + 1) * height, d * share:(d + 1) * share].astype(BF16)
+
+
+def finish(d_heads, weight, normed, x, d_x1, time_ids, freq_ids, gain, small, up_bias_grad, clips, shares):
     total, features = x.shape
+    share = features // shares
+    half = 3 * features // 2
+    wide = half * 2 // 9
     return pl.pallas_call(
-        functools.partial(finish_body, clips),
+        functools.partial(finish_body, clips, shares),
         out_shape=[
             jax.ShapeDtypeStruct((total, features), BF16),
-            jax.ShapeDtypeStruct((features, 3 * features), BF16),
-            jax.ShapeDtypeStruct((SMALL_ROWS, features), F32),
+            jax.ShapeDtypeStruct((shares, 2, 2, share, wide), BF16),
+            jax.ShapeDtypeStruct((shares, 2, share, half - 2 * wide), BF16),
+            jax.ShapeDtypeStruct((shares, 2, SMALL_ROWS // 2, -(-share // 128) * 128), BF16),
         ],
         scratch_shapes=[
             pltpu.VMEM((total, 3 * features), BF16),
             pltpu.VMEM((total, 2 * features), BF16),
-            pltpu.VMEM((8, 128), F32),
+            pltpu.VMEM((SMALL_ROWS, features), F32),
         ],
         compiler_params=params(),
-    )(d_heads, weight, normed, x, d_x1, time_ids, freq_ids, gain, small)
+    )(d_heads, weight, normed, x, d_x1, time_ids, freq_ids, gain, small, up_bias_grad)
+
+
+class Flow:
+    def __init__(self, source, result, refs, place):
+        self.source, self.result = source, result
+        self.split = len(source.shape) == 5
+        self.own, self.got, self.x_got, self.y_got, self.z_got, self.send, self.recv = refs
+        self.z, self.y, self.x, self.c = place
+        self.open = {}
+        if self.split:
+            self.stages = [self.begin, self.cores_x, self.x_y, self.y_z, self.z_fill, self.fill_cores, self.end]
+        else:
+            self.stages = [self.begin, self.cores_y, self.y_z, self.z_x, self.x_cores, self.end]
+        self.used = 0
+
+    def copy(self, key, source, target, peer):
+        z, y, x, c = peer
+        slot = self.used
+        self.used += 1
+        made = pltpu.make_async_remote_copy(
+            src_ref=source, dst_ref=target, send_sem=self.send.at[slot], recv_sem=self.recv.at[slot],
+            device_id=(z * 2 + y, x * 2 + c), device_id_type=pl.DeviceIdType.MESH)
+        made.start()
+        self.open.setdefault(key, []).append(made)
+
+    def wait(self, key):
+        for made in self.open.pop(key):
+            made.wait()
+
+    def at(self, ref, z, y):
+        return ref.at[z * 2 + y, self.x] if self.split else ref.at[z * 2 + y]
+
+    def begin(self):
+        made = pltpu.make_async_copy(self.source.at[:, self.c], self.own, self.send.at[self.used])
+        self.used += 1
+        made.start()
+        self.open["own"] = [made]
+        self.copy("core", self.source.at[:, 1 - self.c], self.got, (self.z, self.y, self.x, 1 - self.c))
+
+    def cores(self):
+        self.wait("own")
+        self.wait("core")
+
+        def add(i, _):
+            self.own[i] = self.own[i] + self.got[i]
+            return 0
+
+        lax.fori_loop(0, self.own.shape[0], add, 0)
+
+    def cores_x(self):
+        self.cores()
+        self.copy("x", self.own.at[:, 1 - self.x], self.x_got, (self.z, self.y, 1 - self.x, self.c))
+
+    def cores_y(self):
+        self.cores()
+        self.to_y()
+
+    def to_y(self):
+        for z in range(4):
+            self.copy("y", self.at(self.own, z, 1 - self.y), self.y_got.at[z], (self.z, 1 - self.y, self.x, self.c))
+
+    def x_y(self):
+        self.wait("x")
+
+        def add(i, _):
+            self.own[i, self.x] = self.own[i, self.x] + self.x_got[i]
+            return 0
+
+        lax.fori_loop(0, self.own.shape[0], add, 0)
+        self.to_y()
+
+    def y_z(self):
+        self.wait("y")
+
+        def add(z, _):
+            spot = self.at(self.own, z, self.y)
+            spot[...] = spot[...] + self.y_got[z]
+            return 0
+
+        lax.fori_loop(0, 4, add, 0)
+        for ahead in range(1, 4):
+            z = lax.rem(self.z + ahead, 4)
+            self.copy("z", self.at(self.own, z, self.y), self.z_got.at[ahead - 1], (z, self.y, self.x, self.c))
+
+    def z_sum(self):
+        self.wait("z")
+        total = self.at(self.own, self.z, self.y)[...].astype(F32)
+        for i in range(3):
+            total = total + self.z_got[i].astype(F32)
+        return total.astype(BF16)
+
+    def z_fill(self):
+        self.result[self.c, self.x] = self.z_sum()
+        spot = self.result.at[self.c, self.x]
+        self.copy("fill", spot, spot, (self.z, self.y, 1 - self.x, self.c))
+
+    def fill_cores(self):
+        self.wait("fill")
+        self.to_core()
+
+    def z_x(self):
+        spot = self.at(self.own, self.z, self.y)
+        spot[...] = self.z_sum()
+        self.copy("x", spot, self.x_got, (self.z, self.y, 1 - self.x, self.c))
+
+    def x_cores(self):
+        self.wait("x")
+        self.result[self.c] = self.at(self.own, self.z, self.y)[...] + self.x_got[...]
+        self.to_core()
+
+    def to_core(self):
+        spot = self.result.at[self.c]
+        self.copy("end", spot, spot, (self.z, self.y, self.x, 1 - self.c))
+
+    def end(self):
+        self.wait("end")
+
+
+def flow_scratch(shape):
+    shares, tail = shape[0], shape[2:]
+    block = tail[-2:]
+    first = (shares,) + block if len(tail) == 3 else block
+    slots = 16
+    return [pltpu.VMEM((shares,) + tail, BF16), pltpu.VMEM((shares,) + tail, BF16), pltpu.VMEM(first, BF16),
+            pltpu.VMEM((4,) + block, BF16), pltpu.VMEM((3,) + block, BF16),
+            pltpu.SemaphoreType.DMA((slots,)), pltpu.SemaphoreType.DMA((slots,))]
+
+
+FLOW_REFS = 7
+
+
+def place_of():
+    d, s = lax.axis_index("dp"), lax.axis_index("seq")
+    return d // 2, d % 2, s // 2, s % 2
+
+
+def greet(place):
+    z, y, x, c = place
+    peers = [(z, y, x, 1 - c), (z, y, 1 - x, c), (z, 1 - y, x, c)] + [(lax.rem(z + i, 4), y, x, c) for i in range(1, 4)]
+    barrier = pltpu.get_barrier_semaphore()
+    for pz, py, px, pc in peers:
+        pl.semaphore_signal(barrier, inc=1, device_id=(pz * 2 + py, px * 2 + pc), device_id_type=pl.DeviceIdType.MESH)
+    pl.semaphore_wait(barrier, len(peers))
+
+
+def reduce_body(count, *refs):
+    sources, results, rest = refs[:count], refs[count:2 * count], refs[2 * count:]
+    place = place_of()
+    greet(place)
+    flows = [Flow(sources[i], results[i], rest[i * FLOW_REFS:(i + 1) * FLOW_REFS], place) for i in range(count)]
+    for level in range(7):
+        for flow in flows:
+            if level < len(flow.stages):
+                flow.stages[level]()
+
+
+def reduce_pieces(pieces):
+    return pl.pallas_call(
+        functools.partial(reduce_body, len(pieces)),
+        in_specs=[pl.BlockSpec(memory_space=pl.ANY)] * len(pieces),
+        out_shape=[jax.ShapeDtypeStruct(p.shape[1:], BF16) for p in pieces],
+        scratch_shapes=[ref for p in pieces for ref in flow_scratch(p.shape)],
+        compiler_params=pltpu.CompilerParams(collective_id=0, has_side_effects=True, vmem_limit_bytes=60 * MIB),
+    )(*pieces)
+
+
+def join_columns(halves, rest):
+    parts = []
+    for core in range(2):
+        parts += [halves[core, 0], halves[core, 1], rest[core]]
+    return jnp.concatenate(parts, 1)
+
+
+def join_rows(halves, rest):
+    parts = []
+    for core in range(2):
+        parts += [halves[core, 0], halves[core, 1], rest[core]]
+    return jnp.concatenate(parts, 0)
+
+
+def collect(down_a, down_b, up_a, up_b, out, qkv_a, qkv_b, packed, finish_part):
+    small = packed.reshape(SMALL_ROWS, packed.shape[2])
+    return (
+        finish_part(join_columns(qkv_a, qkv_b), 0),
+        finish_part(jnp.concatenate([out[0], out[1]], 1), 0),
+        finish_part(join_columns(up_a, up_b), 0),
+        finish_part(join_rows(down_a, down_b), 1).T,
+        finish_part(small, 1),
+    )
 
 
 def exchange(array):
     return lax.all_to_all(array, "seq", split_axis=0, concat_axis=0, tiled=True)
 
 
-def reduce_all(g_qkv, g_out, g_up, g_down_t, small, up_bias_grad):
-    shares = lax.axis_size("dp")
-    features = small.shape[1]
-    hidden = up_bias_grad.shape[1]
+def reduce_all(pieces, custom, features, hidden, time_count, freq_count):
+    if custom:
+        qkv, out, up, down, small = collect(*reduce_pieces(pieces), lambda v, axis: v.astype(F32))
+        small = small[:, 0:features // lax.axis_size("dp")]
+    else:
+        def total(part, axis):
+            return lax.psum(lax.psum_scatter(part, "dp", scatter_dimension=axis, tiled=True), "seq").astype(F32)
+
+        qkv, out, up, down, small = collect(*(p[0] for p in pieces), total)
     repeat = hidden // features
-    chunks = up_bias_grad.reshape(shares, repeat, features // shares)
-    small = small.at[8:8 + repeat].set(jnp.swapaxes(chunks, 0, 1).reshape(repeat, features))
-
-    def total(part, axis):
-        return lax.psum(lax.psum_scatter(part, "dp", scatter_dimension=axis, tiled=True), "seq").astype(F32)
-
-    small = total(small, 1)
-    up_bias = small[8:8 + repeat].reshape(hidden // shares)
+    up_bias = small[8:8 + repeat].reshape(-1)
     return (
-        total(g_qkv, 0), small[0], small[1], total(g_out, 0), small[2], small[3], small[4], small[5], small[6],
-        total(g_up, 0), up_bias, total(g_down_t, 1).T, small[7],
-        small[16:16 + 101], small[16 + FREQ_ROW:16 + FREQ_ROW + 12],
+        qkv, small[0], small[1], out, small[2], small[3], small[4], small[5], small[6], up, up_bias, down, small[7],
+        small[16:16 + time_count], small[16 + FREQ_ROW:16 + FREQ_ROW + freq_count],
     )
 
 
@@ -462,19 +707,23 @@
     mixed, logs = attend(heads, lengths, head_dim, used, used // 4)
     mixed = exchange(mixed)
     x = x.reshape(total, features)
-    output, d_mixed, d_x1, g_down_t, g_up, g_out, small, up_bias_grad = middle(
+    custom = lax.axis_size("dp") == 8 and groups == 4
+    shares = 8 if custom else 1
+    output, d_mixed, d_x1, down_a, down_b, up_a, up_b, g_out, small, up_bias_grad = middle(
         limits, x, mixed.reshape(groups, total, width), cotangent.reshape(total, features), out_weight, line(out_bias),
-        line(norm2_gain), line(norm2_shift), up_weight, line(up_bias), down_weight, line(down_bias), clips, 512
+        line(norm2_gain), line(norm2_shift), up_weight, line(up_bias), down_weight, line(down_bias), clips, up_weight.shape[1] // 4, shares
     )
     d_mixed = exchange(d_mixed.reshape(groups, clips, rows, width))
     d_heads = attend_back(heads, d_mixed, logs, lengths, head_dim, used, 256)
     d_heads = exchange(d_heads)
-    d_patch, g_qkv, small = finish(
+    d_patch, qkv_a, qkv_b, packed = finish(
         d_heads.reshape(groups, total, 3 * width), qkv_weight, normed.reshape(total, features), x, d_x1, time_rows, freq_rows,
-        line(norm1_gain), small, clips
+        line(norm1_gain), small, up_bias_grad, clips, shares
     )
     shape = patches.shape
-    return (output.reshape(shape), d_patch.reshape(shape)) + reduce_all(g_qkv, g_out, g_up, g_down_t, small, up_bias_grad)
+    return (output.reshape(shape), d_patch.reshape(shape)) + reduce_all(
+        (down_a, down_b, up_a, up_b, g_out, qkv_a, qkv_b, packed), custom, features, up_weight.shape[1], time_table.shape[0], freq_table.shape[0]
+    )
 
 
 def solution(mesh):

time: 626 us -> 348 us (0.56)
  waiting for transfers between devices: 352 us -> 12.8 us
  Pallas kernels: 95.9 us -> 189 us
  between operations: 14.3 us -> 0.86 us
  blocking collectives: 122 us -> 110 us
    reduce_scatter x3 -> x0, waiting for transfers between devices: 238 us -> none  [total(): lax.psum_scatter(part, 'dp', scatter_dimension=axis, tiled=True)]
    pallas_call x2 -> x3, Pallas kernels: 49.4 us -> 143 us  [the longest x1 93 us: reduce_pieces(): pl.pallas_call(functools.partial(reduce_body, len(pieces)), in_specs=[pl....]
    unnamed x8 -> x0, waiting for transfers between devices: 67.2 us -> none
    psum x1 -> x0, waiting for transfers between devices: 33.8 us -> none  [total(): lax.psum(lax.psum_scatter(part, 'dp', scatter_dimension=axis, tiled=True)...]
    psum x1 -> x0, blocking collectives: 11.7 us -> none  [total(): lax.psum(lax.psum_scatter(part, 'dp', scatter_dimension=axis, tiled=True)...]
    unnamed x26 -> x34, local copies, waits for them, and re-layouts: 14.8 us -> 6.46 us
  transfers between devices with their start and end apart: 7 -> 1, of which waited for: 6 -> 1; matrix products, arithmetic and copies ran while one was open for 2% -> 1% of each run, Pallas kernels for 5% -> 0%
where the time goes in v2:
time: 348 us; the launch traced here: 347 us
  Pallas kernels  189 us (54%)
  blocking collectives  110 us (32%)
  local copies, waits for them, and re-layouts  25.4 us (7%)
  waiting for transfers between devices  12.8 us (4%)
  other arithmetic  4.96 us (1%)
  starting transfers between devices  3.85 us (1%)
    all_to_all x3, blocking collectives, exchange(): return lax.all_to_all(array, 'seq', split_axis=0, concat_axis=0, tiled=True)  110 us
    pallas_call x1, Pallas kernels, reduce_pieces(): pl.pallas_call(functools.partial(reduce_body, len(pieces)), in_specs=[pl....  93 us
    pallas_call x1, Pallas kernels, middle(): pl.pallas_call(functools.partial(middle_body, clips, shares), grid_spec=p...  36.7 us
    pallas_call x1, Pallas kernels, attend_back(): pl.pallas_call(functools.partial(attend_back_body, used, head_dim, block)...  20.4 us
    pallas_call x1, Pallas kernels, attend(): pl.pallas_call(functools.partial(attend_body, used, head_dim, block), gri...  17.5 us
    pallas_call x1, Pallas kernels, finish(): pl.pallas_call(functools.partial(finish_body, clips, shares), out_shape=[...  13 us
    all_to_all x1, waiting for transfers between devices, exchange(): return lax.all_to_all(array, 'seq', split_axis=0, concat_axis=0, tiled=True)  12.8 us
    pallas_call x1, Pallas kernels, project(): pl.pallas_call(functools.partial(project_body, groups), grid=(clips,), in...  8.43 us
  transfers between devices with their start and end apart: 1, of which 1 were waited for; matrix products, arithmetic and copies ran while one was open for 1% of the time, Pallas kernels for 0%

profile of v2, /device:TPU:0, one launch (start us, length us, event | category | flops | bytes accessed | tf_op | source)
XLA Modules:
  0.0 347.0 jit_solution(12854026572142369032)
XLA Ops:
  0.7 1.3 reshape.95.time_ids
  1.9 1.3 reshape.96.freq_ids
  3.2 1.3 reshape.97.gain
  4.5 1.3 reshape.98.shift
  5.7 0.7 pad_maximum_fusion
  6.5 0.6 reshape.99.bias
  7.1 8.4 %shard_map.323 = (f32[3,224,768]{2,1,0:T(8,128)}, bf16[3,224,768]{2,1,0:T(8,128)(2,1)}, bf16[4,3,224,576]{3,2,1,0:T(8,128)(2,1)}) custom-call(bf16[3,224,768]{2,1,0:T(8,128)(2,1)} %patch.1, s32[3,1,224]{2,1,0:T(1,128)} %reshape.95.time_ids, s32[3,1,224]{2,1,0:T(1,128)} %reshape.96.freq_ids, f32[101,768]{1,0:T(8,128)} %time_table.1, f32[12,768]{1,0:T(8,128)} %freq_table.1, ...), custom_call_target="tpu_custom_call" | custom-call | tf_op jit(solution)/shard_map/pallas_call | solution.py:94
  15.5 46.2 %all_to_all.20.heads = bf16[4,3,224,576]{3,2,1,0:T(8,128)(2,1)} all-to-all(bf16[4,3,224,576]{3,2,1,0:T(8,128)(2,1)} %get-tuple-element.45), channel_id=1, replica_groups=mesh['dp'=8,'seq'=4] {'seq'}, dimensions={0} | all-to-all | bytes 6193152 | tf_op jit(solution)/shard_map/all_to_all | solution.py:650
  61.7 17.5 %shard_map.324 = (bf16[4,3,224,192]{3,2,1,0:T(8,128)(2,1)}, f32[3,8,704]{2,1,0:T(8,128)}) custom-call(s32[3]{0:T(128)} %lengths.3, bf16[4,3,224,576]{3,2,1,0:T(8,128)(2,1)} %all_to_all.20.heads), custom_call_target="tpu_custom_call" | custom-call | tf_op jit(solution)/shard_map/pallas_call | solution.py:148
  79.2 2.5 copy.39
  81.7 0.0 copy-start.8
  81.7 3.9 %all-to-all-start.1 = ((bf16[4,3,224,192]{2,3,1,0:T(8,128)(2,1)}), bf16[4,3,224,192]{2,3,1,0:T(8,128)(2,1)S(1)}, u32[]{:S(2)}, u32[]{:S(2)}) async-start(bf16[4,3,224,192]{2,3,1,0:T(8,128)(2,1)} %copy.39), calls=%async_computation.1 | async-start | bytes 2359296 | tf_op jit(solution)/shard_map/all_to_all | solution.py:650
  85.6 0.0 copy-done.4
  85.6 0.6 reshape.103.out_bias
  86.2 0.0 copy-done.5
  86.2 0.6 reshape.104.gain
  86.7 0.6 reshape.105.shift
  87.3 0.6 reshape.107.down_bias
  87.9 0.0 copy-done.8
  87.9 0.5 broadcast_subtract_fusion.limits
  88.4 12.8 %all-to-all-done.1 = bf16[4,3,224,192]{2,3,1,0:T(8,128)(2,1)S(1)} async-done(((bf16[4,3,224,192]{2,3,1,0:T(8,128)(2,1)}), bf16[4,3,224,192]{2,3,1,0:T(8,128)(2,1)S(1)}, u32[]{:S(2)}, u32[]{:S(2)}) %all-to-all-start.1) | async-done | bytes 1032224 | tf_op jit(solution)/shard_map/all_to_all | solution.py:650
  101.2 1.5 copy.40
  102.7 36.7 %shard_map.325 = (bf16[672,768]{1,0:T(8,128)(2,1)}, bf16[4,672,192]{2,1,0:T(8,128)(2,1)}, f32[672,768]{1,0:T(8,128)}, bf16[8,2,2,96,384]{4,3,2,1,0:T(8,128)(2,1)...) custom-call(s32[3]{0:T(128)} %broadcast_subtract_fusion.limits, ...), custom_call_target="tpu_custom_call" | custom-call | tf_op jit(solution)/shard_map/pallas_call | solution.py:292
  139.4 1.7 copy.41
  141.1 18.3 %all_to_all.21 = bf16[4,3,224,192]{2,3,1,0:T(8,128)(2,1)S(1)} all-to-all(bf16[4,3,224,192]{2,3,1,0:T(8,128)(2,1)S(1)} %copy.41), channel_id=1, replica_groups=mesh['dp'=8,'seq'=4] {'seq'}, dimensions={0} | all-to-all | bytes 2064384 | tf_op jit(solution)/shard_map/all_to_all | solution.py:650
  159.4 1.5 copy.42.d_mixed_in
  160.9 20.4 %shard_map.326 = bf16[4,3,224,576]{3,2,1,0:T(8,128)(2,1)} custom-call(s32[3]{0:T(128)} %lengths.3, bf16[4,3,224,576]{3,2,1,0:T(8,128)(2,1)} %all_to_all.20.heads, bf16[4,3,224,192]{3,2,1,0:T(8,128)(2,1)} %copy.42.d_mixed_in, f32[3,8,704]{2,1,0:T(8,128)} %get-tuple-element.49.logs), custom_call_target="tpu_custom_call" | custom-call | tf_op jit(solution)/shard_map/pallas_call | solution.py:365
  181.3 45.6 %all_to_all.22 = bf16[4,3,224,576]{3,2,1,0:T(8,128)(2,1)} all-to-all(bf16[4,3,224,576]{3,2,1,0:T(8,128)(2,1)} %shard_map.326), channel_id=1, replica_groups=mesh['dp'=8,'seq'=4] {'seq'}, dimensions={0} | all-to-all | bytes 6193152 | tf_op jit(solution)/shard_map/all_to_all | solution.py:650
  226.9 13.0 %shard_map.327 = (bf16[672,768]{1,0:T(8,128)(2,1)}, bf16[8,2,2,96,256]{4,3,2,1,0:T(8,128)(2,1)}, bf16[8,2,96,640]{3,2,1,0:T(8,128)(2,1)}, bf16[8,2,80,128]{3,2,1,0:T(8,128)(2,1)}) custom-call(bf16[4,672,576]{2,1,0:T(8,128)(2,1)} %bitcast.70, bf16[768,2304]{1,0:T(8,128)(2,1)} %weight.3, bf16[672,768]{1,0:T(8,128)(2,1)} %bitcast.76, f32[672,768]{1,0:T(8,128)} %bitcast.72, ...), custom_call_target="tpu_custom_call" | custom-call | tf_op jit(solution)/shard_map/pallas_call | solution.py:443
  239.9 93.0 %shard_map.328 = (bf16[2,2,96,384]{3,2,1,0:T(8,128)(2,1)}, bf16[2,192,384]{2,1,0:T(8,128)(2,1)}, bf16[2,2,96,384]{3,2,1,0:T(8,128)(2,1)}, bf16[2,96,768]{2,1,0:T...) custom-call(bf16[8,2,2,96,384]{4,3,2,1,0:T(8,128)(2,1)} %get-tuple-e, ...), custom_call_target="tpu_custom_call" | custom-call | tf_op jit(solution)/shard_map/pallas_call | solution.py:615
  333.0 0.8 bitcast_convert_fusion
  333.8 0.5 slice_bitcast_fusion.2
  334.4 0.6 slice.146
  335.0 0.7 reshape.113
  335.6 0.7 copy.44
  336.3 1.0 slice_bitcast_fusion.1
  337.3 0.8 bitcast_dynamic-update-slice_fusion.17
  338.1 0.8 bitcast_dynamic-update-slice_fusion.16
  339.0 0.9 bitcast_dynamic-update-slice_fusion.5
  339.9 0.8 bitcast_dynamic-update-slice_fusion.15
  340.7 0.8 bitcast_dynamic-update-slice_fusion.14
  341.5 0.9 bitcast_dynamic-update-slice_fusion.4
  342.4 1.0 convert_element_type.16
  343.5 0.0 copy-done.2
  343.7 1.1 convert_element_type.20
  344.8 0.1 convert_bitcast_fusion
  344.9 1.4 copy.43
  346.3 0.7 maximum_convert_fusion
  (27 shorter events, 0.2 us)
Async XLA Ops:
  81.7 3.9 %copy-start.4 = (f32[768]{0:T(1024)S(1)}, f32[768]{0:T(1024)}, u32[]{:S(2)}) copy-start(f32[768]{0:T(1024)} %param.29) | copy-start | bytes 9220
  81.7 4.5 %copy-start.5 = (f32[768]{0:T(1024)S(1)}, f32[768]{0:T(1024)}, u32[]{:S(2)}) copy-start(f32[768]{0:T(1024)} %param.32) | copy-start | bytes 9220
  81.7 5.1 %copy-start.6 = (f32[768]{0:T(1024)S(1)}, f32[768]{0:T(1024)}, u32[]{:S(2)}) copy-start(f32[768]{0:T(1024)} %param.33) | copy-start | bytes 9220
  81.7 5.6 %copy-start.7 = (f32[768]{0:T(1024)S(1)}, f32[768]{0:T(1024)}, u32[]{:S(2)}) copy-start(f32[768]{0:T(1024)} %param.37) | copy-start | bytes 9220
  81.7 6.2 %copy-start.8 = (s32[3]{0:T(128)S(1)}, s32[3]{0:T(128)}, u32[]{:S(2)}) copy-start(s32[3]{0:T(128)} %lengths.3) | copy-start | bytes 40
  81.7 19.5 %all-to-all-start.1 = ((bf16[4,3,224,192]{2,3,1,0:T(8,128)(2,1)}), bf16[4,3,224,192]{2,3,1,0:T(8,128)(2,1)S(1)}, u32[]{:S(2)}, u32[]{:S(2)}) async-start(bf16[4,3,224,192]{2,3,1,0:T(8,128)(2,1)} %copy.39), calls=%async_computation.1 | async-start | bytes 2359296 | tf_op jit(solution)/shard_map/all_to_all | solution.py:650
  332.9 10.5 %copy-start.3 = (bf16[2,2,96,384]{3,2,1,0:T(8,128)(2,1)S(1)}, bf16[2,2,96,384]{3,2,1,0:T(8,128)(2,1)}, u32[]{:S(2)}) copy-start(bf16[2,2,96,384]{3,2,1,0:T(8,128)(2,1)} %get-tuple-element.67) | copy-start | bytes 884740
  333.0 10.5 %copy-start = (bf16[2,96,768]{2,1,0:T(8,128)(2,1)S(1)}, bf16[2,96,768]{2,1,0:T(8,128)(2,1)}, u32[]{:S(2)}) copy-start(bf16[2,96,768]{2,1,0:T(8,128)(2,1)} %get-tuple-element.68) | copy-start | bytes 884740
  336.3 7.1 %copy-start.2 = (bf16[2,2,96,384]{3,2,1,0:T(8,128)(2,1)S(1)}, bf16[2,2,96,384]{3,2,1,0:T(8,128)(2,1)}, u32[]{:S(2)}) copy-start(bf16[2,2,96,384]{3,2,1,0:T(8,128)(2,1)} %get-tuple-element.69) | copy-start | bytes 884740
  338.1 5.4 %copy-start.1 = (bf16[2,192,384]{2,1,0:T(8,128)(2,1)S(1)}, bf16[2,192,384]{2,1,0:T(8,128)(2,1)}, u32[]{:S(2)}) copy-start(bf16[2,192,384]{2,1,0:T(8,128)(2,1)} %get-tuple-element.70) | copy-start | bytes 884740

commit v3 on v2

v3 whole, which is shorter than its diff:
```python
import functools
import math

import jax
import jax.numpy as jnp
from jax import lax
from jax.experimental import pallas as pl
from jax.experimental.pallas import tpu as pltpu
from jax.sharding import PartitionSpec as P

HEADS = 12
EPS = 1e-06
NEGATIVE = -1000000000.0
FREQ_ROW = 104
TABLE_ROWS = 128
SMALL_ROWS = 32 + TABLE_ROWS
F32 = jnp.float32
BF16 = jnp.bfloat16
NN = (((1,), (0,)), ((), ()))
NT = (((1,), (1,)), ((), ()))
TN = (((0,), (0,)), ((), ()))
MIB = 1 << 20


def mm(left, right, dims=NN):
    return lax.dot_general(left, right, dims, preferred_element_type=F32)


def params(limit=60):
    return pltpu.CompilerParams(vmem_limit_bytes=limit * MIB)


def row_sum(values):
    return jnp.sum(values, 0, keepdims=True)


def normalize(values):
    center = values - jnp.mean(values, -1, keepdims=True)
    rstd = lax.rsqrt(jnp.mean(center * center, -1, keepdims=True) + EPS)
    return center * rstd, rstd


def norm_back(d_out, gain, xhat, rstd):
    u = d_out * gain
    inner = jnp.mean(u * xhat, -1, keepdims=True)
    return rstd * (u - jnp.mean(u, -1, keepdims=True) - xhat * inner)


def split_high_low(values):
    high = values.astype(BF16)
    return high, (values - high.astype(F32)).astype(BF16)


def one_hot(time_row, freq_row):
    spot = lax.broadcasted_iota(jnp.int32, (TABLE_ROWS, time_row.shape[1]), 0)
    hit = (spot == time_row) | (spot == freq_row + FREQ_ROW)
    return jnp.where(hit, 1.0, 0.0).astype(BF16)


ROWS = 224
OWN = 352
SHARED = 176
WORK = OWN + SHARED
KEYS = 2 * OWN
SHARED_MOVES = (
    (0, 2, 176, 48, 3, 384), (1, 2, 176, 48, 3, 432), (2, 2, 176, 48, 3, 480), (3, 2, 0, 32, 3, 352),
    (0, 2, 0, 176, 0, 352), (1, 2, 0, 176, 1, 352), (2, 2, 0, 176, 2, 352),
)
OWN_MOVES = (
    (2, 0, 0, 128, 0, 224), (2, 0, 128, 96, 1, 224), (3, 0, 0, 32, 1, 320), (0, 1, 0, 224, 2, 0), (1, 1, 0, 224, 3, 0),
    (2, 1, 128, 96, 3, 224), (2, 1, 0, 128, 2, 224), (3, 1, 0, 32, 3, 320), (0, 0, 0, 224, 0, 0), (1, 0, 0, 224, 1, 0),
)
MOVES = SHARED_MOVES + OWN_MOVES
UNUSED = (3, 32)


def seq_place():
    s = lax.axis_index("seq")
    return s, s // 2, lax.rem(s, 2)


def seq_peer(s):
    return {"seq": s}


def greet_group(s):
    barrier = pltpu.get_barrier_semaphore()
    for ahead in range(1, 4):
        pl.semaphore_signal(barrier, inc=1, device_id=seq_peer(lax.rem(s + ahead, 4)), device_id_type=pl.DeviceIdType.MESH)
    pl.semaphore_wait(barrier, 3)


class Mover:
    def __init__(self, s, at_home, at_work, send, recv, back=False):
        self.s, self.at_home, self.at_work, self.send, self.recv, self.back = s, at_home, at_work, send, recv, back

    def ends(self, move):
        home, clip, first, count, work, spot = move
        a, b = self.at_home.at[clip, pl.ds(first, count)], self.at_work.at[pl.ds(spot, count)]
        return (work, b, home, a) if self.back else (home, a, work, b)

    def each(self, moves, which, act, near=True):
        for device in range(4):
            chosen = [m for m in moves if self.ends(m)[which] == device and (near or self.ends(m)[0] != self.ends(m)[2])]
            if not chosen:
                continue

            @pl.when(self.s == device)
            def _(chosen=chosen):
                for m in chosen:
                    src_device, src, dst_device, dst = self.ends(m)
                    slot = MOVES.index(m)
                    if src_device == dst_device:
                        act(False, pltpu.make_async_copy(src, dst, self.recv.at[slot]))
                    else:
                        act(True, pltpu.make_async_remote_copy(
                            src_ref=src, dst_ref=dst, send_sem=self.send.at[slot], recv_sem=self.recv.at[slot],
                            device_id=seq_peer(dst_device), device_id_type=pl.DeviceIdType.MESH))

    def start(self, moves):
        self.each(moves, 0, lambda far, made: made.start())

    def wait(self, moves):
        self.each(moves, 2, lambda far, made: made.wait_recv() if far else made.wait())

    def drain(self, moves):
        self.each(moves, 0, lambda far, made: made.wait_send(), False)


class Sender:
    def __init__(self, send, recv):
        self.send, self.recv, self.used = send, recv, 0

    def far(self, source, target, peer):
        made = pltpu.make_async_remote_copy(
            src_ref=source, dst_ref=target, send_sem=self.send.at[self.used], recv_sem=self.recv.at[self.used],
            device_id=seq_peer(peer), device_id_type=pl.DeviceIdType.MESH)
        self.used += 1
        made.start()
        return made

    def near(self, source, target):
        made = pltpu.make_async_copy(source, target, self.recv.at[self.used])
        self.used += 1
        made.start()
        return made


def wait_all(copies):
    for made in copies:
        made.wait()


def shift_between(spot, cuts):
    slot = spot
    for low, high, shift in cuts:
        slot = jnp.where((spot >= low) & (spot < high), spot + shift, slot)
    return slot


def own_slots(spot):
    return shift_between(spot, ((224, 352, 224), (352, 576, -128)))


def shared_slots(spot):
    return shift_between(spot, ((176, 352, 48), (352, 528, 96), (528, 560, 144), (560, 608, -384), (608, 656, -208), (656, 704, -32)))


def span(first, size):
    return pl.ds(pl.multiple_of(first, 16), size)


def attend(query, keys, values, key_ok, mixed_out, log_out, log_wide, head_dim):
    count = query.shape[1]
    lane = lax.broadcasted_iota(jnp.int32, (1, 128), 1) // head_dim
    wide = lax.broadcasted_iota(jnp.int32, (SHARED, 128), 1)
    scale = BF16(1.0 / math.sqrt(head_dim))

    def pair(p, _):
        k, v = keys[p], values[p]
        for first in range(0, count, SHARED):
            q = query[p, first:first + SHARED] * scale
            mixed = jnp.zeros((SHARED, 128), F32)
            logs = jnp.zeros((SHARED, 128), F32)
            for h in range(128 // head_dim):
                scores = jnp.where(key_ok, mm(jnp.where(lane == h, q, BF16(0)), k, NT), NEGATIVE)
                highest = jnp.max(scores, -1, keepdims=True)
                powers = jnp.exp(scores - highest)
                total = jnp.sum(powers, -1, keepdims=True)
                out = mm(powers.astype(BF16), v) * (1.0 / total)
                mixed = jnp.where(lane == h, out, mixed)
                logs = jnp.where(wide == h, highest + jnp.log(total), logs)
            mixed_out[p, first:first + SHARED] = mixed.astype(BF16)
            log_wide[first:first + SHARED] = logs
        log_out[p] = log_wide[0:count].T[0:8]
        return 0

    lax.fori_loop(0, query.shape[0], pair, 0)


def forward_body(head_dim, lengths, patches, cot, time_ids, freq_ids, time_table, freq_table, gain, shift, weight, query_bias, value_bias,
                 x_out, n_out, own_out, shared_q_out, shared_kv_out, own_log, shared_log, mixed_out, cot_out, id_out, valid_out,
                 work, table_f32, table, ids, matrix, own_stage, shared_stage, own_mixed, shared_mixed, log_wide,
                 patch_send, patch_recv, cot_send, cot_recv, send, recv, weight_sem):
    s, x, c = seq_place()
    features = x_out.shape[1]
    groups = own_out.shape[1]
    other = 1 - c
    loads = [pltpu.make_async_copy(weight.at[:, pl.ds(p * features, features)], matrix.at[:, pl.ds(p * features, features)], weight_sem.at[p])
             for p in range(3)]
    for load in loads:
        load.start()
    greet_group(s)
    patch_mover = Mover(s, patches, work, patch_send, patch_recv)
    cot_mover = Mover(s, cot, cot_out, cot_send, cot_recv)
    sender = Sender(send, recv)
    id_copies = []
    for i, source in enumerate((time_ids, freq_ids)):
        id_copies.append(sender.near(source, ids.at[s, i]))
        for ahead in range(1, 4):
            id_copies.append(sender.far(source, ids.at[s, i], lax.rem(s + ahead, 4)))
    patch_mover.start(MOVES)

    table_f32[...] = jnp.zeros_like(table_f32)
    table_f32[0:time_table.shape[0], :] = time_table[...]
    table_f32[FREQ_ROW:FREQ_ROW + freq_table.shape[0], :] = freq_table[...]
    high, low = split_high_low(table_f32[...])
    table[0:TABLE_ROWS, :] = high
    table[TABLE_ROWS:, :] = low
    spot = lax.broadcasted_iota(jnp.int32, (WORK, 1), 0)
    place = jnp.where(spot < OWN, jnp.where(spot < ROWS, spot + ROWS * c, spot + ROWS + 128 * c), shared_slots(spot - OWN + SHARED * s))
    limit = jnp.where(spot < OWN, jnp.where(x == 0, lengths[0], lengths[1]), lengths[2])
    valid_out[...] = jnp.broadcast_to(jnp.where(place < limit, 1.0, 0.0), valid_out.shape)
    id_out[...] = jnp.zeros_like(id_out)
    wait_all(id_copies)
    for device in range(4):
        @pl.when(s == device)
        def _(device=device):
            for home, clip, first, count, target, at in MOVES:
                if target == device:
                    for i in range(2):
                        id_out[i:i + 1, at:at + count] = ids[home, i, clip:clip + 1, first:first + count]

    bias = (query_bias[...].reshape(1, features), None, value_bias[...].reshape(1, features))

    def project(first, stage, at):
        rows = slice(first, first + SHARED)
        hot = one_hot(id_out[0:1, rows], id_out[1:2, rows])
        value = work[rows].astype(F32) + mm(jnp.concatenate([hot, hot], 0), table[...], TN)
        x_out[rows] = value
        xhat, _ = normalize(value)
        normed = (xhat * gain[...].reshape(1, features) + shift[...].reshape(1, features)).astype(BF16)
        n_out[rows] = normed
        for part in range(3):
            out = mm(normed, matrix[:, part * features:(part + 1) * features])
            if bias[part] is not None:
                out = out + bias[part]
            out = out.astype(BF16)
            for g in range(2 * groups):
                stage[part, g, at:at + SHARED] = out[:, g * 128:(g + 1) * 128]

    patch_mover.wait(SHARED_MOVES)
    wait_all(loads)
    project(OWN, shared_stage, 0)
    q_rows, kv_rows = span(SHARED * c, SHARED), span(SHARED * s, SHARED)
    mine, theirs = pl.ds(groups * c, groups), pl.ds(groups * other, groups)
    partner, across, diagonal = 2 * x + other, 2 * (1 - x) + c, 2 * (1 - x) + other
    shared_copies = [
        sender.far(shared_stage.at[0, theirs], shared_q_out.at[:, q_rows], partner),
        sender.far(shared_stage.at[1:3, theirs], shared_kv_out.at[:, :, kv_rows], partner),
        sender.far(shared_stage.at[1:3, mine], shared_kv_out.at[:, :, kv_rows], across),
        sender.far(shared_stage.at[1:3, theirs], shared_kv_out.at[:, :, kv_rows], diagonal),
        sender.near(shared_stage.at[0, mine], shared_q_out.at[:, q_rows]),
        sender.near(shared_stage.at[1:3, mine], shared_kv_out.at[:, :, kv_rows]),
    ]
    patch_mover.wait(OWN_MOVES)
    project(0, own_stage, 0)
    project(SHARED, own_stage, SHARED)
    own_rows = span(OWN * c, OWN)
    own_copies = [
        sender.far(own_stage.at[:, theirs], own_out.at[:, :, own_rows], partner),
        sender.near(own_stage.at[:, mine], own_out.at[:, :, own_rows]),
    ]
    cot_mover.start(MOVES)
    wait_all(own_copies)
    key_spot = lax.broadcasted_iota(jnp.int32, (1, KEYS), 1)
    attend(own_out.at[0], own_out.at[1], own_out.at[2], own_slots(key_spot) < jnp.where(x == 0, lengths[0], lengths[1]),
           own_mixed, own_log, log_wide, head_dim)
    mixed_copies = [
        sender.far(own_mixed.at[:, span(OWN * other, OWN)], mixed_out.at[mine, 0:OWN], partner),
        sender.near(own_mixed.at[:, own_rows], mixed_out.at[mine, 0:OWN]),
    ]
    wait_all(shared_copies)
    attend(shared_q_out, shared_kv_out.at[0], shared_kv_out.at[1], shared_slots(key_spot) < lengths[2],
           shared_mixed, shared_log, log_wide, head_dim)
    mixed_copies += [
        sender.far(shared_mixed.at[:, span(SHARED * other, SHARED)], mixed_out.at[mine, OWN:WORK], partner),
        sender.near(shared_mixed.at[:, q_rows], mixed_out.at[mine, OWN:WORK]),
    ]
    wait_all(mixed_copies)
    cot_mover.wait(MOVES)
    patch_mover.drain(MOVES)
    cot_mover.drain(MOVES)


def forward(lengths, patches, cot, time_ids, freq_ids, time_table, freq_table, gain, shift, weight, query_bias, value_bias, head_dim):
    features = patches.shape[2]
    groups = features // 256
    anywhere, vmem = pl.BlockSpec(memory_space=pl.ANY), pl.BlockSpec(memory_space=pltpu.VMEM)
    lanes = lambda *lead: jax.ShapeDtypeStruct(lead + (128,), BF16)
    dma = pltpu.SemaphoreType.DMA
    return pl.pallas_call(
        functools.partial(forward_body, head_dim),
        in_specs=[pl.BlockSpec(memory_space=pltpu.SMEM)] + [anywhere] * 4 + [vmem] * 4 + [anywhere] + [vmem] * 2,
        out_specs=[vmem] * 8 + [anywhere] + [vmem] * 2,
        out_shape=[
            jax.ShapeDtypeStruct((WORK, features), F32),
            jax.ShapeDtypeStruct((WORK, features), BF16),
            lanes(3, groups, KEYS),
            lanes(groups, OWN),
            lanes(2, groups, KEYS),
            jax.ShapeDtypeStruct((groups, 8, KEYS), F32),
            jax.ShapeDtypeStruct((groups, 8, OWN), F32),
            lanes(2 * groups, WORK),
            jax.ShapeDtypeStruct((WORK, features), BF16),
            jax.ShapeDtypeStruct((8, WORK), jnp.int32),
            jax.ShapeDtypeStruct((WORK, 128), F32),
        ],
        scratch_shapes=[
            pltpu.VMEM((WORK, features), BF16),
            pltpu.VMEM((TABLE_ROWS, features), F32),
            pltpu.VMEM((2 * TABLE_ROWS, features), BF16),
            pltpu.VMEM((4, 2) + time_ids.shape, jnp.int32),
            pltpu.VMEM(weight.shape, BF16),
            pltpu.VMEM((3, 2 * groups, OWN, 128), BF16),
            pltpu.VMEM((3, 2 * groups, SHARED, 128), BF16),
            pltpu.VMEM((groups, KEYS, 128), BF16),
            pltpu.VMEM((groups, OWN, 128), BF16),
            pltpu.VMEM((KEYS, 128), F32),
            dma((len(MOVES),)), dma((len(MOVES),)), dma((len(MOVES),)), dma((len(MOVES),)), dma((24,)), dma((24,)), dma((3,)),
        ],
        compiler_params=pltpu.CompilerParams(collective_id=1, has_side_effects=True, vmem_limit_bytes=60 * MIB),
    )(lengths, patches, cot, time_ids, freq_ids, time_table, freq_table, gain, shift, weight, query_bias, value_bias)


def middle_body(blocks, shares, valid, x_in, mixed_in, cot, out_weight, out_bias, gain, shift, up, up_bias, down, down_bias,
                out_ref, d_mixed_ref, d_x1_ref, g_down_a, g_down_b, g_up_a, g_up_b, g_out, small, up_bias_grad,
                mixed, x1, n2, n2_t, dm, dm_t, acc, d_n2, act_all, d_hidden_all):
    step = pl.program_id(0)
    groups, total, width = mixed_in.shape
    rows = total // blocks
    features = x_in.shape[1]
    share = features // shares

    flat = lambda ref: ref[...].reshape(1, ref.shape[0])

    @pl.when(step == 0)
    def _():
        small[...] = jnp.zeros_like(small)
        for c in range(blocks):
            span = slice(c * rows, (c + 1) * rows)
            for g in range(groups):
                mixed[span, g * width:(g + 1) * width] = mixed_in[g, span, :]
            after = x_in[span] + (mm(mixed[span], out_weight[...]) + flat(out_bias))
            x1[span] = after
            xhat, _ = normalize(after)
            n2[span] = (xhat * flat(gain) + flat(shift)).astype(BF16)
            dm[span] = (cot[span].astype(F32) * valid[span, 0:1]).astype(BF16)
        n2_t[...] = n2[...].T
        dm_t[...] = dm[...].T
        acc[...] = jnp.zeros_like(acc)
        d_n2[...] = jnp.zeros_like(d_n2)
        small[7:8, :] = row_sum(dm[...].astype(F32))

    tile_bias = up_bias[pl.ds(pl.multiple_of(step * up.shape[1], 128), up.shape[1])].reshape(1, up.shape[1])
    bias_sum = None
    for c in range(blocks):
        span = slice(c * rows, (c + 1) * rows)
        hidden = mm(n2[span], up[...]) + tile_bias
        half = 0.5 * (1.0 + lax.erf(hidden * (1.0 / math.sqrt(2.0))))
        act = (hidden * half).astype(BF16)
        slope = half + hidden * jnp.exp(hidden * hidden * -0.5) * (1.0 / math.sqrt(2.0 * math.pi))
        d_hidden = (slope * mm(dm[span], down[...], NT)).astype(BF16)
        act_all[span] = act
        d_hidden_all[span] = d_hidden
        acc[span] += mm(act, down[...])
        d_n2[span] += mm(d_hidden, up[...], NT)
        part = row_sum(d_hidden.astype(F32))
        bias_sum = part if bias_sum is None else bias_sum + part
    up_bias_grad[...] = bias_sum
    tile = up.shape[1]
    heights = g_down_a.shape[3], g_down_b.shape[2]
    reach = g_down_a.shape[4]
    for core in range(2):
        first = core * (features // 2)
        out = mm(dm_t[first:first + features // 2], act_all[...]).astype(BF16)
        for d in range(tile // reach):
            cols = slice(d * reach, (d + 1) * reach)
            for half_x in range(2):
                g_down_a[d, core, half_x] = out[half_x * heights[0]:(half_x + 1) * heights[0], cols]
            g_down_b[d, core] = out[2 * heights[0]:, cols]
    g_up_tile = mm(n2_t[...], d_hidden_all[...]).astype(BF16)

    @pl.when(step % 2 == 0)
    def _():
        wide = tile // 2
        for d in range(shares):
            for half_x in range(2):
                g_up_a[d, 0, half_x] = g_up_tile[d * share:(d + 1) * share, half_x * wide:(half_x + 1) * wide]

    @pl.when(step % 2 == 1)
    def _():
        for d in range(shares):
            g_up_b[d, 0] = g_up_tile[d * share:(d + 1) * share]

    @pl.when(step == pl.num_programs(0) - 1)
    def _():
        gain_sum = jnp.zeros((1, features), F32)
        shift_sum = jnp.zeros((1, features), F32)
        bias_out = jnp.zeros((1, features), F32)
        for c in range(blocks):
            span = slice(c * rows, (c + 1) * rows)
            ok = valid[span, 0:1]
            after = x1[span]
            out_ref[span] = (ok * (after + (acc[span] + flat(down_bias)))).astype(BF16)
            xhat, rstd = normalize(after)
            d_norm = d_n2[span]
            gain_sum += row_sum(d_norm * xhat)
            shift_sum += row_sum(d_norm)
            d_x1 = dm[span].astype(F32) + norm_back(d_norm, flat(gain), xhat, rstd)
            d_x1_ref[span] = d_x1
            d_a = d_x1.astype(BF16)
            n2[span] = d_a
            bias_out += row_sum(d_a.astype(F32))
            d_mixed = mm(d_a, out_weight[...], NT).astype(BF16)
            for g in range(groups):
                d_mixed_ref[g, span, :] = d_mixed[:, g * width:(g + 1) * width]
        out = mm(mixed[...].T, n2[...]).astype(BF16)
        for d in range(shares):
            for core in range(2):
                g_out[d, core] = out[d * share:(d + 1) * share, core * (features // 2):(core + 1) * (features // 2)]
        small[2:3, :] = bias_out
        small[5:6, :] = gain_sum
        small[6:7, :] = shift_sum


def middle(valid, x, mixed, cot, out_weight, out_bias, gain, shift, up, up_bias, down, down_bias, blocks, tile, shares):
    total, features = x.shape
    groups, _, width = mixed.shape
    hidden = up.shape[1]
    share, reach, half = features // shares, hidden // shares, features // 2
    spread = max(tile // reach, 1)
    whole = lambda a: pl.BlockSpec(a.shape, lambda j: (0,) * len(a.shape))
    outs = [
        jax.ShapeDtypeStruct((total, features), BF16),
        jax.ShapeDtypeStruct((groups, total, width), BF16),
        jax.ShapeDtypeStruct((total, features), F32),
        jax.ShapeDtypeStruct((shares, 2, 2, half // 4, reach), BF16),
        jax.ShapeDtypeStruct((shares, 2, half // 2, reach), BF16),
        jax.ShapeDtypeStruct((shares, 2, 2, share, hidden // 8), BF16),
        jax.ShapeDtypeStruct((shares, 2, share, hidden // 4), BF16),
        jax.ShapeDtypeStruct((shares, 2, share, half), BF16),
        jax.ShapeDtypeStruct((8, features), F32),
        jax.ShapeDtypeStruct((1, hidden), F32),
    ]
    cols = lambda height: pl.BlockSpec((height, tile), lambda j: (0, j))
    if tile >= reach:
        down_spec = lambda *mid: pl.BlockSpec((spread,) + mid + (reach,), lambda j: (j,) + (0,) * (len(mid) + 1))
    else:
        down_spec = lambda *mid: pl.BlockSpec((1,) + mid + (tile,), lambda j: (0,) * (len(mid) + 1) + (j,))
    return pl.pallas_call(
        functools.partial(middle_body, blocks, shares),
        grid_spec=pl.GridSpec(
            grid=(hidden // tile,),
            in_specs=[whole(valid), whole(x), whole(mixed), whole(cot), whole(out_weight), whole(out_bias), whole(gain), whole(shift),
                      cols(features), whole(up_bias), pl.BlockSpec((tile, features), lambda j: (j, 0)), whole(down_bias)],
            out_specs=[whole(outs[0]), whole(outs[1]), whole(outs[2]), down_spec(2, 2, half // 4), down_spec(2, half // 2),
                       pl.BlockSpec((shares, 1, 2, share, tile // 2), lambda j: (0, j // 2, 0, 0, 0)),
                       pl.BlockSpec((shares, 1, share, tile), lambda j: (0, j // 2, 0, 0)),
                       whole(outs[7]), whole(outs[8]), cols(1)],
            scratch_shapes=[
                pltpu.VMEM((total, features), BF16),
                pltpu.VMEM((total, features), F32),
                pltpu.VMEM((total, features), BF16),
                pltpu.VMEM((features, total), BF16),
                pltpu.VMEM((total, features), BF16),
                pltpu.VMEM((features, total), BF16),
                pltpu.VMEM((total, features), F32),
                pltpu.VMEM((total, features), F32),
                pltpu.VMEM((total, tile), BF16),
                pltpu.VMEM((total, tile), BF16),
            ],
        ),
        out_shape=outs,
        compiler_params=params(),
    )(valid, x, mixed, cot, out_weight, out_bias, gain, shift, up, up_bias, down, down_bias)


def attend_back(query, keys, values, d_mixed, logs, key_ok, d_query, d_keys, d_values, head_dim, block):
    count = query.shape[1]
    lane = lax.broadcasted_iota(jnp.int32, (1, 128), 1) // head_dim
    scale = BF16(1.0 / math.sqrt(head_dim))

    def pair(p, _):
        k, v = keys[p], values[p]
        k_t = (k * scale).T
        total_k = jnp.zeros((KEYS, 128), F32)
        total_v = jnp.zeros((KEYS, 128), F32)
        for first in range(0, count, block):
            last = min(first + block, count)
            q_block = query[p, first:last] * scale
            m_block = d_mixed[p, first:last]
            parts = []
            for h in range(128 // head_dim):
                q_head = jnp.where(lane == h, q_block, BF16(0))
                m_head = jnp.where(lane == h, m_block, BF16(0))
                scores = jnp.where(key_ok, mm(k, q_head, NT), NEGATIVE)
                probs = jnp.exp(scores - logs[p, h:h + 1, first:last])
                total_v = total_v + mm(probs.astype(BF16), m_head)
                weighted = probs * mm(v, m_head, NT)
                d_scores = (weighted - probs * row_sum(weighted)).astype(BF16)
                total_k = total_k + mm(d_scores, q_head)
                parts.append(mm(k_t[h * head_dim:(h + 1) * head_dim], d_scores))
            d_query[p, first:last] = jnp.concatenate(parts, 0).T.astype(BF16)
        d_keys[p] = total_k.astype(BF16)
        d_values[p] = total_v.astype(BF16)
        return 0

    lax.fori_loop(0, query.shape[0], pair, 0)


def backward_body(head_dim, shares, lengths, d_mixed, own, shared_q, shared_kv, own_log, shared_log, weight, normed, x_in, d_x1, ids, gain,
                  small_in, up_bias_grad, out_work,
                  output, d_patches, g_qkv_a, g_qkv_b, packed,
                  own_dm, shared_dm, own_d, shared_dq, shared_dkv, other_dkv, joined_lanes, joined, d_work, high_low, small, zeros, matrix,
                  out_send, out_recv, d_send, d_recv, send, recv, weight_sem, zero_sem):
    s, x, c = seq_place()
    total, features = x_in.shape
    groups = own.shape[1]
    other = 1 - c
    partner, across = 2 * x + other, 2 * (1 - x) + c
    mine, theirs = pl.ds(groups * c, groups), pl.ds(groups * other, groups)
    own_rows, q_rows = span(OWN * c, OWN), span(SHARED * c, SHARED)
    load = pltpu.make_async_copy(weight, matrix, weight_sem.at[0])
    load.start()
    zeros[...] = jnp.zeros_like(zeros)
    greet_group(s)
    sender = Sender(send, recv)
    shared_copies = [
        sender.far(d_mixed.at[theirs, OWN:WORK], shared_dm.at[:, q_rows], partner),
        sender.near(d_mixed.at[mine, OWN:WORK], shared_dm.at[:, q_rows]),
    ]
    own_copies = [
        sender.far(d_mixed.at[theirs, 0:OWN], own_dm.at[:, own_rows], partner),
        sender.near(d_mixed.at[mine, 0:OWN], own_dm.at[:, own_rows]),
    ]
    out_mover = Mover(s, output, out_work, out_send, out_recv, True)
    d_mover = Mover(s, d_patches, d_work, d_send, d_recv, True)

    def fill(act):
        @pl.when(s == UNUSED[0])
        def _():
            for i, array in enumerate((output, d_patches)):
                for clip in range(3):
                    act(pltpu.make_async_copy(zeros, array.at[clip, pl.ds(UNUSED[1], ROWS - UNUSED[1])], zero_sem.at[3 * i + clip]))

    fill(lambda made: made.start())
    key_spot = lax.broadcasted_iota(jnp.int32, (KEYS, 1), 0)
    wait_all(shared_copies)
    attend_back(shared_q, shared_kv.at[0], shared_kv.at[1], shared_dm, shared_log, shared_slots(key_spot) < lengths[2],
                shared_dq, shared_dkv.at[0], shared_dkv.at[1], head_dim, 256)
    kv_copy = sender.far(shared_dkv.at[:, :, span(OWN * (1 - x), OWN)], other_dkv, across)
    out_mover.start(MOVES)
    wait_all(own_copies)
    attend_back(own.at[0], own.at[1], own.at[2], own_dm, own_log, own_slots(key_spot) < jnp.where(x == 0, lengths[0], lengths[1]),
                own_d.at[0], own_d.at[1], own_d.at[2], head_dim, 256)
    own_copies = [
        sender.far(own_d.at[:, :, span(OWN * other, OWN)], joined_lanes.at[:, mine, 0:OWN], partner),
        sender.near(own_d.at[:, :, own_rows], joined_lanes.at[:, mine, 0:OWN]),
    ]
    kv_copy.wait()
    for i in range(2):
        for g in range(groups):
            rows = span(OWN * x, OWN)
            shared_dkv[i, g, rows] = shared_dkv[i, g, rows] + other_dkv[i, g]
    shared_copies = []
    for to, peer in ((other, partner), (c, None)):
        q_part = shared_dq.at[:, span(SHARED * to, SHARED)]
        kv_part = shared_dkv.at[:, :, span(OWN * x + SHARED * to, SHARED)]
        q_place, kv_place = joined_lanes.at[0, mine, OWN:WORK], joined_lanes.at[1:3, mine, OWN:WORK]
        if peer is None:
            shared_copies += [sender.near(q_part, q_place), sender.near(kv_part, kv_place)]
        else:
            shared_copies += [sender.far(q_part, q_place, peer), sender.far(kv_part, kv_place, peer)]
    load.wait()
    small[0:8, :] = small_in[...]
    small[8:, :] = jnp.zeros((small.shape[0] - 8, features), F32)
    sums = [jnp.zeros((1, features), F32)] * 4
    tables = jnp.zeros((TABLE_ROWS, 2 * features), F32)
    wait_all(own_copies)
    for first in range(0, total, SHARED):
        if first == OWN:
            wait_all(shared_copies)
        rows = slice(first, first + SHARED)
        for part in range(3):
            for g in range(2 * groups):
                at = (part * 2 * groups + g) * 128
                joined[rows, at:at + 128] = joined_lanes[part, g, rows]
        d_norm = mm(joined[rows], matrix[...], NT)
        xhat, rstd = normalize(x_in[rows])
        terms = (joined[rows, 0:features].astype(F32), joined[rows, 2 * features:].astype(F32), d_norm * xhat, d_norm)
        sums = [a + row_sum(b) for a, b in zip(sums, terms)]
        d_x = d_x1[rows] + norm_back(d_norm, gain[...].reshape(1, features), xhat, rstd)
        high, low = split_high_low(d_x)
        d_work[rows] = high
        tables = tables + mm(one_hot(ids[0:1, rows], ids[1:2, rows]), jnp.concatenate([high, low], 1))
        if first + SHARED == OWN:
            d_mover.start(OWN_MOVES)
    d_mover.start(SHARED_MOVES)
    normed_t = normed[...].T
    half = 3 * features // 2
    wide = g_qkv_a.shape[4]
    share = features // shares
    for core in range(2):
        out = mm(normed_t, joined[:, core * half:(core + 1) * half]).astype(BF16)
        for d in range(shares):
            rows = slice(d * share, (d + 1) * share)
            for half_x in range(2):
                g_qkv_a[d, core, half_x] = out[rows, half_x * wide:(half_x + 1) * wide]
            g_qkv_b[d, core] = out[rows, 2 * wide:]
    small[16:16 + TABLE_ROWS, :] = tables[:, 0:features] + tables[:, features:]
    for row, value in zip((0, 1, 3, 4), sums):
        small[row:row + 1, :] = value
    repeat = up_bias_grad.shape[1] // features
    height = packed.shape[2]
    if share != packed.shape[3]:
        packed[...] = jnp.zeros_like(packed)
    for d in range(shares):
        for r in range(repeat):
            first = (d * repeat + r) * share
            small[8 + r:9 + r, d * share:(d + 1) * share] = up_bias_grad[:, first:first + share]
        for core in range(2):
            packed[d, core, :, 0:share] = small[core * height:(core + 1) * height, d * share:(d + 1) * share].astype(BF16)
    out_mover.wait(MOVES)
    d_mover.wait(MOVES)
    out_mover.drain(MOVES)
    d_mover.drain(MOVES)
    fill(lambda made: made.wait())


def backward(lengths, d_mixed, own, shared_q, shared_kv, own_log, shared_log, weight, normed, x, d_x1, ids, gain, small, up_bias_grad, out_work,
             head_dim, shares):
    total, features = x.shape
    groups = own.shape[1]
    share = features // shares
    half = 3 * features // 2
    wide = half * 2 // 9
    anywhere, vmem = pl.BlockSpec(memory_space=pl.ANY), pl.BlockSpec(memory_space=pltpu.VMEM)
    dma = pltpu.SemaphoreType.DMA
    lanes = lambda *lead: pltpu.VMEM(lead + (128,), BF16)
    moves = len(MOVES)
    return pl.pallas_call(
        functools.partial(backward_body, head_dim, shares),
        in_specs=[pl.BlockSpec(memory_space=pltpu.SMEM), anywhere] + [vmem] * 5 + [anywhere] + [vmem] * 7 + [anywhere],
        out_specs=[anywhere] * 2 + [vmem] * 3,
        out_shape=[
            jax.ShapeDtypeStruct((3, ROWS, features), BF16),
            jax.ShapeDtypeStruct((3, ROWS, features), BF16),
            jax.ShapeDtypeStruct((shares, 2, 2, share, wide), BF16),
            jax.ShapeDtypeStruct((shares, 2, share, half - 2 * wide), BF16),
            jax.ShapeDtypeStruct((shares, 2, SMALL_ROWS // 2, -(-share // 128) * 128), BF16),
        ],
        scratch_shapes=[
            lanes(groups, KEYS), lanes(groups, OWN), lanes(3, groups, KEYS), lanes(groups, OWN), lanes(2, groups, KEYS), lanes(2, groups, OWN),
            lanes(3, 2 * groups, WORK),
            pltpu.VMEM((total, 3 * features), BF16),
            pltpu.VMEM((total, features), BF16),
            pltpu.VMEM((8, 128), BF16),
            pltpu.VMEM((SMALL_ROWS, features), F32),
            pltpu.VMEM((ROWS - UNUSED[1], features), BF16),
            pltpu.VMEM(weight.shape, BF16),
            dma((moves,)), dma((moves,)), dma((moves,)), dma((moves,)), dma((16,)), dma((16,)), dma((1,)), dma((6,)),
        ],
        compiler_params=pltpu.CompilerParams(collective_id=2, has_side_effects=True, vmem_limit_bytes=60 * MIB),
    )(lengths, d_mixed, own, shared_q, shared_kv, own_log, shared_log, weight, normed, x, d_x1, ids, gain, small, up_bias_grad, out_work)


class Flow:
    def __init__(self, source, result, refs, place):
        self.source, self.result = source, result
        self.split = len(source.shape) == 5
        self.own, self.got, self.x_got, self.y_got, self.z_got, self.send, self.recv = refs
        self.z, self.y, self.x, self.c = place
        self.open = {}
        if self.split:
            self.stages = [self.begin, self.cores_x, self.x_y, self.y_z, self.z_fill, self.fill_cores, self.end]
        else:
            self.stages = [self.begin, self.cores_y, self.y_z, self.z_x, self.x_cores, self.end]
        self.used = 0

    def copy(self, key, source, target, peer):
        z, y, x, c = peer
        slot = self.used
        self.used += 1
        made = pltpu.make_async_remote_copy(
            src_ref=source, dst_ref=target, send_sem=self.send.at[slot], recv_sem=self.recv.at[slot],
            device_id=(z * 2 + y, x * 2 + c), device_id_type=pl.DeviceIdType.MESH)
        made.start()
        self.open.setdefault(key, []).append(made)

    def wait(self, key):
        for made in self.open.pop(key):
            made.wait()

    def at(self, ref, z, y):
        return ref.at[z * 2 + y, self.x] if self.split else ref.at[z * 2 + y]

    def begin(self):
        made = pltpu.make_async_copy(self.source.at[:, self.c], self.own, self.send.at[self.used])
        self.used += 1
        made.start()
        self.open["own"] = [made]
        self.copy("core", self.source.at[:, 1 - self.c], self.got, (self.z, self.y, self.x, 1 - self.c))

    def cores(self):
        self.wait("own")
        self.wait("core")

        def add(i, _):
            self.own[i] = self.own[i] + self.got[i]
            return 0

        lax.fori_loop(0, self.own.shape[0], add, 0)

    def cores_x(self):
        self.cores()
        self.copy("x", self.own.at[:, 1 - self.x], self.x_got, (self.z, self.y, 1 - self.x, self.c))

    def cores_y(self):
        self.cores()
        self.to_y()

    def to_y(self):
        for z in range(4):
            self.copy("y", self.at(self.own, z, 1 - self.y), self.y_got.at[z], (self.z, 1 - self.y, self.x, self.c))

    def x_y(self):
        self.wait("x")

        def add(i, _):
            self.own[i, self.x] = self.own[i, self.x] + self.x_got[i]
            return 0

        lax.fori_loop(0, self.own.shape[0], add, 0)
        self.to_y()

    def y_z(self):
        self.wait("y")

        def add(z, _):
            spot = self.at(self.own, z, self.y)
            spot[...] = spot[...] + self.y_got[z]
            return 0

        lax.fori_loop(0, 4, add, 0)
        for ahead in range(1, 4):
            z = lax.rem(self.z + ahead, 4)
            self.copy("z", self.at(self.own, z, self.y), self.z_got.at[ahead - 1], (z, self.y, self.x, self.c))

    def z_sum(self):
        self.wait("z")
        total = self.at(self.own, self.z, self.y)[...].astype(F32)
        for i in range(3):
            total = total + self.z_got[i].astype(F32)
        return total.astype(BF16)

    def z_fill(self):
        self.result[self.c, self.x] = self.z_sum()
        spot = self.result.at[self.c, self.x]
        self.copy("fill", spot, spot, (self.z, self.y, 1 - self.x, self.c))

    def fill_cores(self):
        self.wait("fill")
        self.to_core()

    def z_x(self):
        spot = self.at(self.own, self.z, self.y)
        spot[...] = self.z_sum()
        self.copy("x", spot, self.x_got, (self.z, self.y, 1 - self.x, self.c))

    def x_cores(self):
        self.wait("x")
        self.result[self.c] = self.at(self.own, self.z, self.y)[...] + self.x_got[...]
        self.to_core()

    def to_core(self):
        spot = self.result.at[self.c]
        self.copy("end", spot, spot, (self.z, self.y, self.x, 1 - self.c))

    def end(self):
        self.wait("end")


def flow_scratch(shape):
    shares, tail = shape[0], shape[2:]
    block = tail[-2:]
    first = (shares,) + block if len(tail) == 3 else block
    slots = 16
    return [pltpu.VMEM((shares,) + tail, BF16), pltpu.VMEM((shares,) + tail, BF16), pltpu.VMEM(first, BF16),
            pltpu.VMEM((4,) + block, BF16), pltpu.VMEM((3,) + block, BF16),
            pltpu.SemaphoreType.DMA((slots,)), pltpu.SemaphoreType.DMA((slots,))]


FLOW_REFS = 7


def place_of():
    d, s = lax.axis_index("dp"), lax.axis_index("seq")
    return d // 2, d % 2, s // 2, s % 2


def greet(place):
    z, y, x, c = place
    peers = [(z, y, x, 1 - c), (z, y, 1 - x, c), (z, 1 - y, x, c)] + [(lax.rem(z + i, 4), y, x, c) for i in range(1, 4)]
    barrier = pltpu.get_barrier_semaphore()
    for pz, py, px, pc in peers:
        pl.semaphore_signal(barrier, inc=1, device_id=(pz * 2 + py, px * 2 + pc), device_id_type=pl.DeviceIdType.MESH)
    pl.semaphore_wait(barrier, len(peers))


def reduce_body(count, *refs):
    sources, results, rest = refs[:count], refs[count:2 * count], refs[2 * count:]
    place = place_of()
    greet(place)
    flows = [Flow(sources[i], results[i], rest[i * FLOW_REFS:(i + 1) * FLOW_REFS], place) for i in range(count)]
    for level in range(7):
        for flow in flows:
            if level < len(flow.stages):
                flow.stages[level]()


def reduce_pieces(pieces):
    return pl.pallas_call(
        functools.partial(reduce_body, len(pieces)),
        in_specs=[pl.BlockSpec(memory_space=pl.ANY)] * len(pieces),
        out_shape=[jax.ShapeDtypeStruct(p.shape[1:], BF16) for p in pieces],
        scratch_shapes=[ref for p in pieces for ref in flow_scratch(p.shape)],
        compiler_params=pltpu.CompilerParams(collective_id=0, has_side_effects=True, vmem_limit_bytes=60 * MIB),
    )(*pieces)


def join_columns(halves, rest):
    parts = []
    for core in range(2):
        parts += [halves[core, 0], halves[core, 1], rest[core]]
    return jnp.concatenate(parts, 1)


def join_rows(halves, rest):
    parts = []
    for core in range(2):
        parts += [halves[core, 0], halves[core, 1], rest[core]]
    return jnp.concatenate(parts, 0)


def collect(down_a, down_b, up_a, up_b, out, qkv_a, qkv_b, packed, finish_part):
    small = packed.reshape(SMALL_ROWS, packed.shape[2])
    return (
        finish_part(join_columns(qkv_a, qkv_b), 0),
        finish_part(jnp.concatenate([out[0], out[1]], 1), 0),
        finish_part(join_columns(up_a, up_b), 0),
        finish_part(join_rows(down_a, down_b), 1).T,
        finish_part(small, 1),
    )


def reduce_all(pieces, custom, features, hidden, time_count, freq_count):
    if custom:
        qkv, out, up, down, small = collect(*reduce_pieces(pieces), lambda v, axis: v.astype(F32))
        small = small[:, 0:features // lax.axis_size("dp")]
    else:
        def total(part, axis):
            return lax.psum(lax.psum_scatter(part, "dp", scatter_dimension=axis, tiled=True), "seq").astype(F32)

        qkv, out, up, down, small = collect(*(p[0] for p in pieces), total)
    repeat = hidden // features
    up_bias = small[8:8 + repeat].reshape(-1)
    return (
        qkv, small[0], small[1], out, small[2], small[3], small[4], small[5], small[6], up, up_bias, down, small[7],
        small[16:16 + time_count], small[16 + FREQ_ROW:16 + FREQ_ROW + freq_count],
    )


def shards(
    patches,
    cotangent,
    time_ids,
    freq_ids,
    lengths,
    qkv_weight,
    query_bias,
    value_bias,
    out_weight,
    out_bias,
    norm1_gain,
    norm1_shift,
    norm2_gain,
    norm2_shift,
    up_weight,
    up_bias,
    down_weight,
    down_bias,
    time_table,
    freq_table,
):
    features = patches.shape[2]
    head_dim = features // HEADS
    assert patches.shape[:2] == (3, ROWS) and lax.axis_size("seq") == 4
    custom = lax.axis_size("dp") == 8
    shares = 8 if custom else 1
    x, normed, own, shared_q, shared_kv, own_log, shared_log, mixed, cot, ids, valid = forward(
        lengths, patches, cotangent, time_ids, freq_ids, time_table, freq_table, norm1_gain, norm1_shift, qkv_weight, query_bias, value_bias,
        head_dim
    )
    out_work, d_mixed, d_x1, down_a, down_b, up_a, up_b, g_out, small, up_bias_grad = middle(
        valid, x, mixed, cot, out_weight, out_bias, norm2_gain, norm2_shift, up_weight, up_bias, down_weight, down_bias, 3,
        up_weight.shape[1] // 4, shares
    )
    output, d_patch, qkv_a, qkv_b, packed = backward(
        lengths, d_mixed, own, shared_q, shared_kv, own_log, shared_log, qkv_weight, normed, x, d_x1, ids, norm1_gain, small, up_bias_grad,
        out_work, head_dim, shares
    )
    return (output, d_patch) + reduce_all(
        (down_a, down_b, up_a, up_b, g_out, qkv_a, qkv_b, packed), custom, features, up_weight.shape[1], time_table.shape[0],
        freq_table.shape[0]
    )


def solution(mesh):
    clip_spec, row_spec, one = P("dp", "seq", None), P("dp", "seq"), P("dp")
    matrix = P("dp", None)
    return jax.shard_map(
        shards,
        mesh=mesh,
        in_specs=(clip_spec, clip_spec, row_spec, row_spec, one) + (P(),) * 15,
        out_specs=(clip_spec, clip_spec, matrix, one, one, matrix, one, one, one, one, one, matrix, one, matrix, one, P(None, "dp"), P(None, "dp")),
        check_vma=False,
    )
```

time: 348 us -> 231 us (0.66)
  blocking collectives: 110 us -> 0 us
  Pallas kernels: 189 us -> 214 us
  local copies, waits for them, and re-layouts: 25.4 us -> 11.8 us
  waiting for transfers between devices: 12.8 us -> 0 us
  starting transfers between devices: 3.85 us -> 0 us
    all_to_all x3 -> x0, blocking collectives: 110 us -> none  [exchange(): return lax.all_to_all(array, 'seq', split_axis=0, concat_axis=0, tiled=True)]
    pallas_call x5 -> x3, Pallas kernels: 96.1 us -> 122 us  [the longest x1 49 us: backward(): pl.pallas_call(functools.partial(backward_body, head_dim, shares), in_spe...]
    all_to_all x1 -> x0, waiting for transfers between devices: 12.8 us -> none  [exchange(): return lax.all_to_all(array, 'seq', split_axis=0, concat_axis=0, tiled=True)]
    reshape x10 -> x0, local copies, waits for them, and re-layouts: 9.7 us -> none  [the longest x7 5.48 us: shards(): line = lambda v: v.reshape(1, -1)]
    all_to_all x1 -> x0, starting transfers between devices: 3.85 us -> none  [exchange(): return lax.all_to_all(array, 'seq', split_axis=0, concat_axis=0, tiled=True)]
    unnamed x34 -> x32, local copies, waits for them, and re-layouts: 6.46 us -> 9 us
  transfers between devices with their start and end apart: 1 -> 0, of which waited for: 1 -> 0; matrix products, arithmetic and copies ran while one was open for 1% -> 0% of each run, Pallas kernels for 0% -> 0%
where the time goes in v3:
time: 231 us; the launch traced here: 230 us
  Pallas kernels  214 us (93%)
  local copies, waits for them, and re-layouts  11.8 us (5%)
  other arithmetic  3.73 us (2%)
    pallas_call x1, Pallas kernels, reduce_pieces(): pl.pallas_call(functools.partial(reduce_body, len(pieces)), in_specs=[pl....  92.1 us
    pallas_call x1, Pallas kernels, backward(): pl.pallas_call(functools.partial(backward_body, head_dim, shares), in_spe...  49 us
    pallas_call x1, Pallas kernels, forward(): pl.pallas_call(functools.partial(forward_body, head_dim), in_specs=[pl.Bl...  38.7 us
    pallas_call x1, Pallas kernels, middle(): pl.pallas_call(functools.partial(middle_body, blocks, shares), grid_spec=...  34.1 us
    unnamed x32, local copies, waits for them, and re-layouts  9 us

profile of v3, /device:TPU:0, one launch (start us, length us, event | category | flops | bytes accessed | tf_op | source)
XLA Modules:
  0.0 230.3 jit_solution(2992267205987602546)
XLA Ops:
  0.7 38.7 %shard_map.323 = (f32[528,768]{1,0:T(8,128)}, bf16[528,768]{1,0:T(8,128)(2,1)}, bf16[3,3,704,128]{3,2,1,0:T(8,128)(2,1)}, bf16[3,352,128]{2,1,0:T(8,128)(2,1)}, ...) custom-call(s32[3]{0:T(128)} %lengths.3, ...), custom_call_target="tpu_custom_call" | custom-call | tf_op jit(solution)/shard_map/pallas_call | solution.py:312
  39.3 34.1 %shard_map.324 = (bf16[528,768]{1,0:T(8,128)(2,1)}, bf16[6,528,128]{2,1,0:T(8,128)(2,1)}, f32[528,768]{1,0:T(8,128)}, bf16[8,2,2,96,384]{4,3,2,1,0:T(8,128)(2,1)...) custom-call(f32[528,128]{1,0:T(8,128)} %get-tuple-element.51.valid, ...), custom_call_target="tpu_custom_call" | custom-call | tf_op jit(solution)/shard_map/pallas_call | solution.py:471
  73.5 49.0 %shard_map.325 = (bf16[3,224,768]{2,1,0:T(8,128)(2,1)}, bf16[3,224,768]{2,1,0:T(8,128)(2,1)}, bf16[8,2,2,96,256]{4,3,2,1,0:T(8,128)(2,1)}, bf16[8,2,96,640]{3,2,1,0:T(8,128)(2,1)}, bf16[8,2,80,128]{3,2,1,0:T(8,128)(2,1)}) custom-call(s32[3]{0:T(128)} %lengths.3, bf16[6,528,128]{2,1,0:T(8,128)(2,1)} %get-tuple-element.55.d_mixed, ...), custom_call_target="tpu_custom_call" | custom-call | tf_op jit(solution)/shard_map/pallas_call | solution.py:662
  122.5 92.1 %shard_map.326 = (bf16[2,2,96,384]{3,2,1,0:T(8,128)(2,1)}, bf16[2,192,384]{2,1,0:T(8,128)(2,1)}, bf16[2,2,96,384]{3,2,1,0:T(8,128)(2,1)}, bf16[2,96,768]{2,1,0:T...) custom-call(bf16[8,2,2,96,384]{4,3,2,1,0:T(8,128)(2,1)} %get-tuple-e, ...), custom_call_target="tpu_custom_call" | custom-call | tf_op jit(solution)/shard_map/pallas_call | solution.py:843
  214.6 0.0 copy-start.6
  214.6 0.8 bitcast_convert_fusion
  215.5 0.0 copy-start.5
  215.5 0.7 reshape.40
  216.1 0.5 slice_bitcast_fusion.2
  216.7 0.6 slice.146
  217.3 0.7 copy.38
  218.0 0.0 copy-start.2
  218.0 1.0 slice_bitcast_fusion.1
  219.0 0.0 copy-start.4
  219.0 0.7 maximum_convert_fusion
  219.7 0.0 copy-start.3
  219.7 0.8 bitcast_dynamic-update-slice_fusion.17
  220.6 0.8 bitcast_dynamic-update-slice_fusion.16
  221.4 0.9 bitcast_dynamic-update-slice_fusion.5
  222.3 0.8 bitcast_dynamic-update-slice_fusion.15
  223.1 0.8 bitcast_dynamic-update-slice_fusion.14
  223.9 0.0 copy-done.6
  223.9 1.0 convert_element_type.16
  224.9 0.0 copy-done.5
  224.9 0.0 copy-done.2
  225.0 0.0 copy-done.4
  225.0 0.0 copy-done.3
  225.2 1.1 convert_element_type.20
  226.3 0.1 convert_bitcast_fusion
  226.4 0.0 copy-start.1
  226.4 1.4 copy.37
  227.8 0.0 copy-done.1
  227.8 0.0 copy-start
  227.8 1.0 copy.56
  228.8 0.6 copy-done
  229.4 1.0 copy.57
  (14 shorter events, 0.2 us)
Async XLA Ops:
  214.6 9.3 %copy-start.6 = (bf16[2,96,640]{2,1,0:T(8,128)(2,1)S(1)}, bf16[2,96,640]{2,1,0:T(8,128)(2,1)}, u32[]{:S(2)}) copy-start(bf16[2,96,640]{2,1,0:T(8,128)(2,1)} %get-tuple-element.78) | copy-start | bytes 737284
  215.5 9.4 %copy-start.5 = (bf16[2,2,96,384]{3,2,1,0:T(8,128)(2,1)S(1)}, bf16[2,2,96,384]{3,2,1,0:T(8,128)(2,1)}, u32[]{:S(2)}) copy-start(bf16[2,2,96,384]{3,2,1,0:T(8,128)(2,1)} %get-tuple-element.81) | copy-start | bytes 884740
  218.0 6.9 %copy-start.2 = (bf16[2,96,768]{2,1,0:T(8,128)(2,1)S(1)}, bf16[2,96,768]{2,1,0:T(8,128)(2,1)}, u32[]{:S(2)}) copy-start(bf16[2,96,768]{2,1,0:T(8,128)(2,1)} %get-tuple-element.82) | copy-start | bytes 884740
  219.0 6.0 %copy-start.4 = (bf16[2,2,96,384]{3,2,1,0:T(8,128)(2,1)S(1)}, bf16[2,2,96,384]{3,2,1,0:T(8,128)(2,1)}, u32[]{:S(2)}) copy-start(bf16[2,2,96,384]{3,2,1,0:T(8,128)(2,1)} %get-tuple-element.83) | copy-start | bytes 884740
  219.7 5.3 %copy-start.3 = (bf16[2,192,384]{2,1,0:T(8,128)(2,1)S(1)}, bf16[2,192,384]{2,1,0:T(8,128)(2,1)}, u32[]{:S(2)}) copy-start(bf16[2,192,384]{2,1,0:T(8,128)(2,1)} %get-tuple-element.84) | copy-start | bytes 884740
  226.4 1.4 copy-start.1
  227.8 1.6 copy-start
